TPU v7x, 128 devices: a whole 4x4x4 slice. The times are simulated.
128 devices in a mesh: dp: 16 (over x, z), mp: 8 (over y, core).
Axes of the slice: x: 4, y: 4, z: 4, core: 2. Of those that a mesh axis runs over, the one named last changes fastest.
Arguments:
- inputs: int32 [64, 512], P('dp'), may hold values from 0 to 255
- targets: int32 [64, 512], P('dp'), may hold values from 0 to 255
- valid_mask: int32 [64, 512], P('dp'), may hold values from 0 to 1
- memory: bfloat16 [2, 64, 512, 512], P(None, 'dp'), may hold values from -6 to 6
- attention_rank: int32 [2, 5, 8, 8], P(None, None, None, 'mp'), may hold values from 0 to 9
- feedforward_rank: int32 [2, 2, 8, 32], P(None, None, None, 'mp'), may hold values from 0 to 9
- attention_weight: float32 [2, 5, 512, 512], P(None, None, None, 'mp'), may hold values from -0.25 to 0.25
- attention_moment: float32 [2, 5, 512, 512], P(None, None, None, 'mp'), may hold values from -0.0034179688 to 0.0034179688
- attention_average: float32 [2, 5, 512, 512], P(None, None, None, 'mp'), may hold values from -0.25 to 0.25
- feedforward_weight: float32 [2, 2, 512, 2048], P(None, None, None, 'mp'), may hold values from -0.625 to 0.625
- feedforward_moment: float32 [2, 2, 512, 2048], P(None, None, None, 'mp'), may hold values from -0.0034179688 to 0.0034179688
- feedforward_average: float32 [2, 2, 512, 2048], P(None, None, None, 'mp'), may hold values from -0.625 to 0.625
- embedding_weight: float32 [256, 512], replicated, may hold values from -8 to 8
- embedding_moment: float32 [256, 512], replicated, may hold values from -0.0034179688 to 0.0034179688
- embedding_average: float32 [256, 512], replicated, may hold values from -8 to 8
- head_bias_weight: float32 [2, 2, 512], P(None, None, 'mp'), may hold values from -1.75 to 1.75
- head_bias_moment: float32 [2, 2, 512], P(None, None, 'mp'), may hold values from -0.0034179688 to 0.0034179688
- head_bias_average: float32 [2, 2, 512], P(None, None, 'mp'), may hold values from -1.75 to 1.75
- inner_bias_weight: float32 [2, 2048], P(None, 'mp'), may hold values from -0.625 to 0.625
- inner_bias_moment: float32 [2, 2048], P(None, 'mp'), may hold values from -0.0034179688 to 0.0034179688
- inner_bias_average: float32 [2, 2048], P(None, 'mp'), may hold values from -0.625 to 0.625
- norm_weight: float32 [2, 5, 512], replicated, as said below
- norm_moment: float32 [2, 5, 512], replicated, may hold values from -0.0034179688 to 0.0034179688
- norm_average: float32 [2, 5, 512], replicated, may hold values from -3 to 3
Outputs:
- ce_total: float32 [], replicated
- valid_count: float32 [], replicated
- new_memory: bfloat16 [2, 64, 512, 512], P(None, 'dp')
- attention_grad: float32 [2, 5, 512, 512], P(None, None, None, 'mp')
- attention_next: float32 [2, 5, 512, 512], P(None, None, None, 'mp')
- attention_moment_next: float32 [2, 5, 512, 512], P(None, None, None, 'mp')
- attention_average_next: float32 [2, 5, 512, 512], P(None, None, None, 'mp')
- feedforward_grad: float32 [2, 2, 512, 2048], P(None, None, None, 'mp')
- feedforward_next: float32 [2, 2, 512, 2048], P(None, None, None, 'mp')
- feedforward_moment_next: float32 [2, 2, 512, 2048], P(None, None, None, 'mp')
- feedforward_average_next: float32 [2, 2, 512, 2048], P(None, None, None, 'mp')
- embedding_next: float32 [256, 512], replicated
- embedding_moment_next: float32 [256, 512], replicated
- embedding_average_next: float32 [256, 512], replicated
- head_bias_next: float32 [2, 2, 512], P(None, None, 'mp')
- head_bias_moment_next: float32 [2, 2, 512], P(None, None, 'mp')
- head_bias_average_next: float32 [2, 2, 512], P(None, None, 'mp')
- inner_bias_next: float32 [2, 2048], P(None, 'mp')
- inner_bias_moment_next: float32 [2, 2048], P(None, 'mp')
- inner_bias_average_next: float32 [2, 2048], P(None, 'mp')
- norm_grad: float32 [2, 5, 512], replicated
- norm_next: float32 [2, 5, 512], replicated
- norm_moment_next: float32 [2, 5, 512], replicated
- norm_average_next: float32 [2, 5, 512], replicated
Inputs may be any that keep to these rules, and one draw needn't show every extreme that they name: `norm_weight`: rows 0 and 2 of each layer are gains near 1, the others offsets and biases of both signs.
All inputs are finite; a program needn't handle non-finite values.
Results may differ from a plain program's by a relative error of at most 0.011.
Values may be sent and summed in bfloat16 or wider, within the bound.
A program may use at most 192 MiB of HBM per device.

v0:
```python
import jax
import jax.numpy as jnp
from jax import lax
from jax.sharding import PartitionSpec as P

HD = 64


PRECISE = lax.Precision.HIGHEST
EPSILON = 1e-05
MOMENTUM = 0.9
AVERAGE = 0.9
RATE = 0.3
PENALTY = 0.0001
WIDEN = 5.0
HALF_TYPE = jnp.bfloat16


def forward_dot(left_side, right_side):
    return jnp.dot(left_side, right_side, preferred_element_type=jnp.float32)


def weight_dot(left_side, right_side):
    return lax.dot_general(
        left_side, right_side, (((0,), (0,)), ((), ())), preferred_element_type=jnp.float32
    )


def back_dot(left_side, right_side):
    return lax.dot_general(
        left_side, right_side, (((1,), (1,)), ((), ())), preferred_element_type=jnp.float32
    )


def smooth_unit(value):
    return (
        0.5
        * value
        * (1.0 + jnp.tanh(0.7978845608028654 * (value + 0.044715 * value * value * value)))
    )


def positions(key_length, model_width):
    distance = jnp.arange(key_length).astype(jnp.float32)
    frequency = 1.0 / 10000.0 ** (jnp.arange(0, model_width, 2).astype(jnp.float32) / model_width)
    angles = distance[:, None] * frequency[None, :]
    return jnp.concatenate([jnp.sin(angles), jnp.cos(angles)], axis=1)


def expand(block_rank, block_size):
    return jnp.repeat(jnp.repeat(block_rank, block_size, axis=-2), block_size, axis=-1).astype(
        jnp.float32
    )


def norm_forward(values, norm_gain, norm_offset):
    centred = values - jnp.mean(values, axis=-1, keepdims=True)
    inverse = lax.rsqrt(jnp.mean(centred * centred, axis=-1, keepdims=True) + EPSILON)
    normed = centred * inverse
    return (normed * norm_gain + norm_offset, normed, inverse)


def norm_backward(grad_output, normed, inverse, norm_gain):
    scaled = grad_output * norm_gain
    grad_input = inverse * (
        scaled
        - jnp.mean(scaled, axis=-1, keepdims=True)
        - normed * jnp.mean(scaled * normed, axis=-1, keepdims=True)
    )
    return (grad_input, jnp.sum(grad_output * normed, 0), jnp.sum(grad_output, 0))


def enter_rows(rows_local):
    low_rows = rows_local.astype(HALF_TYPE)
    return low_rows


def leave_rows(partial_value):
    return lax.psum(partial_value, "mp")


def enter_back(partial_value):
    return lax.psum(partial_value, "mp")


def skew_rows(table_part):
    heads_here, query_count, key_count = table_part.shape
    padded = jnp.pad(table_part, ((0, 0), (0, 0), (0, 1)))
    flat = padded.reshape(heads_here, query_count * (key_count + 1))
    return flat[:, query_count - 1 : query_count - 1 + query_count * key_count].reshape(
        heads_here, query_count, key_count
    )


def unskew_rows(grad_scores):
    heads_here, query_count, key_count = grad_scores.shape
    flat = grad_scores.reshape(heads_here, query_count * key_count)
    padded = jnp.pad(flat, ((0, 0), (query_count - 1, 1)))
    return padded.reshape(heads_here, query_count, key_count + 1)[:, :, :key_count]


def score_block(query_u, query_w, key_rows, rel_reversed, allowed):
    direct = jnp.einsum("she,khe->hsk", query_u, key_rows, preferred_element_type=jnp.float32)
    table_part = jnp.einsum(
        "she,dhe->hsd", query_w, rel_reversed, preferred_element_type=jnp.float32
    )
    score_scale = query_u.shape[-1] ** (-0.5)
    return jnp.where(allowed, (direct + skew_rows(table_part)) * score_scale, -1e30)


def attend_forward(segment_item, rel_reversed, allowed):
    query_u, query_w, key_rows, value_rows = segment_item
    scores = score_block(query_u, query_w, key_rows, rel_reversed, allowed)
    row_peak = jnp.max(scores, axis=-1, keepdims=True)
    log_total = row_peak + jnp.log(jnp.sum(jnp.exp(scores - row_peak), axis=-1, keepdims=True))
    probabilities = jnp.exp(scores - log_total).astype(HALF_TYPE)
    mixed = jnp.einsum(
        "hsk,khe->she", probabilities, value_rows, preferred_element_type=jnp.float32
    )
    return (mixed.astype(HALF_TYPE), log_total)


def attend_backward(segment_item, rel_reversed, allowed):
    query_u, query_w, key_rows, value_rows, log_total, grad_mixed = segment_item
    score_scale = query_u.shape[-1] ** (-0.5)
    scores = score_block(query_u, query_w, key_rows, rel_reversed, allowed)
    probabilities = jnp.exp(scores - log_total)
    grad_probs = jnp.einsum(
        "she,khe->hsk", grad_mixed, value_rows, preferred_element_type=jnp.float32
    )
    grad_scores = (
        probabilities * (grad_probs - jnp.sum(probabilities * grad_probs, axis=-1, keepdims=True))
    ).astype(HALF_TYPE)
    grad_u = (
        jnp.einsum("hsk,khe->she", grad_scores, key_rows, preferred_element_type=jnp.float32)
        * score_scale
    ).astype(HALF_TYPE)
    grad_keys = (
        jnp.einsum("hsk,she->khe", grad_scores, query_u, preferred_element_type=jnp.float32)
        * score_scale
    ).astype(HALF_TYPE)
    grad_table = unskew_rows(grad_scores)
    grad_w = (
        jnp.einsum("hsd,dhe->she", grad_table, rel_reversed, preferred_element_type=jnp.float32)
        * score_scale
    ).astype(HALF_TYPE)
    grad_rel = (
        jnp.einsum("hsd,she->dhe", grad_table, query_w, preferred_element_type=jnp.float32)
        * score_scale
    )[::-1]
    grad_values = jnp.einsum(
        "hsk,she->khe",
        probabilities.astype(HALF_TYPE),
        grad_mixed,
        preferred_element_type=jnp.float32,
    ).astype(HALF_TYPE)
    return (grad_u, grad_w, grad_keys, grad_values, grad_rel.astype(HALF_TYPE))


def layer_forward(
    hidden,
    memory_low,
    attention_eff,
    head_bias,
    feedforward_eff,
    inner_bias,
    norm_set,
    table_low,
    allowed,
):
    segment_count, memory_length, model_width = memory_low.shape
    local_width = attention_eff.shape[2]
    local_heads = local_width // HD
    hidden_low = enter_rows(hidden)
    rows_all = hidden_low.shape[0]
    segment_length = rows_all // segment_count
    raw_query = forward_dot(hidden_low, attention_eff[0])
    query_u = (
        (raw_query + head_bias[0])
        .astype(HALF_TYPE)
        .reshape(segment_count, segment_length, local_heads, HD)
    )
    query_w = (
        (raw_query + head_bias[1])
        .astype(HALF_TYPE)
        .reshape(segment_count, segment_length, local_heads, HD)
    )
    memory_flat = memory_low.reshape(segment_count * memory_length, model_width)

    def joined_rows(weight):
        from_memory = (
            forward_dot(memory_flat, weight)
            .astype(HALF_TYPE)
            .reshape(segment_count, memory_length, local_heads, HD)
        )
        from_hidden = (
            forward_dot(hidden_low, weight)
            .astype(HALF_TYPE)
            .reshape(segment_count, segment_length, local_heads, HD)
        )
        return jnp.concatenate([from_memory, from_hidden], axis=1)

    key_rows = joined_rows(attention_eff[1])
    value_rows = joined_rows(attention_eff[2])
    rel_rows = (
        forward_dot(table_low, attention_eff[3]).astype(HALF_TYPE).reshape(-1, local_heads, HD)
    )
    rel_reversed = rel_rows[::-1]
    mixed, log_total = lax.map(
        lambda segment_item: attend_forward(segment_item, rel_reversed, allowed),
        (query_u, query_w, key_rows, value_rows),
    )
    mixed_flat = mixed.reshape(rows_all, local_width)
    attended = leave_rows(back_dot(mixed_flat, attention_eff[4]))
    middle, normed_one, inverse_one = norm_forward(hidden + attended, norm_set[0], norm_set[1])
    middle_low = enter_rows(middle)
    inner_pre = forward_dot(middle_low, feedforward_eff[0]) + inner_bias
    active = smooth_unit(inner_pre).astype(HALF_TYPE)
    branch = leave_rows(back_dot(active, feedforward_eff[1])) + norm_set[4]
    output, normed_two, inverse_two = norm_forward(middle + branch, norm_set[2], norm_set[3])
    saved_state = (
        hidden_low,
        query_u,
        query_w,
        key_rows,
        value_rows,
        rel_reversed,
        log_total,
        mixed_flat,
        normed_one,
        inverse_one,
        middle_low,
        inner_pre,
        active,
        normed_two,
        inverse_two,
    )
    return (output, saved_state)


def layer_backward(
    grad_output,
    saved_state,
    memory_low,
    attention_eff,
    feedforward_eff,
    norm_set,
    table_low,
    allowed,
):
    (
        hidden_low,
        query_u,
        query_w,
        key_rows,
        value_rows,
        rel_reversed,
        log_total,
        mixed_flat,
        normed_one,
        inverse_one,
        middle_low,
        inner_pre,
        active,
        normed_two,
        inverse_two,
    ) = saved_state
    segment_count, memory_length, model_width = memory_low.shape
    rows_all, local_width = mixed_flat.shape
    grad_sum_two, grad_gain_two, grad_offset_two = norm_backward(
        grad_output, normed_two, inverse_two, norm_set[2]
    )
    grad_branch = grad_sum_two.astype(HALF_TYPE)
    grad_down = weight_dot(grad_branch, active)
    grad_active = forward_dot(grad_branch, feedforward_eff[1])
    unit_value, unit_back = jax.vjp(smooth_unit, inner_pre)
    grad_inner = unit_back(grad_active)[0].astype(HALF_TYPE)
    grad_up = weight_dot(middle_low, grad_inner)
    grad_middle = grad_sum_two + enter_back(back_dot(grad_inner, feedforward_eff[0]))
    grad_sum_one, grad_gain_one, grad_offset_one = norm_backward(
        grad_middle, normed_one, inverse_one, norm_set[0]
    )
    grad_attended = grad_sum_one.astype(HALF_TYPE)
    grad_out_proj = weight_dot(grad_attended, mixed_flat)
    grad_mixed = (
        forward_dot(grad_attended, attention_eff[4]).astype(HALF_TYPE).reshape(query_u.shape)
    )
    grad_u, grad_w, grad_keys, grad_values, grad_rel = lax.map(
        lambda segment_item: attend_backward(segment_item, rel_reversed, allowed),
        (query_u, query_w, key_rows, value_rows, log_total, grad_mixed),
    )
    grad_u_flat = grad_u.astype(jnp.float32).reshape(rows_all, local_width)
    grad_w_flat = grad_w.astype(jnp.float32).reshape(rows_all, local_width)
    grad_query = (grad_u_flat + grad_w_flat).astype(HALF_TYPE)
    grad_bias = jnp.stack([jnp.sum(grad_u_flat, 0), jnp.sum(grad_w_flat, 0)])

    def split_rows(grad_rows):
        shaped = grad_rows.reshape(segment_count, -1, local_width)
        return (
            shaped[:, :memory_length].reshape(segment_count * memory_length, local_width),
            shaped[:, memory_length:].reshape(rows_all, local_width),
        )

    key_memory, key_hidden = split_rows(grad_keys)
    value_memory, value_hidden = split_rows(grad_values)
    memory_flat = memory_low.reshape(segment_count * memory_length, model_width)
    grad_query_w = weight_dot(hidden_low, grad_query)
    grad_key_w = weight_dot(memory_flat, key_memory) + weight_dot(hidden_low, key_hidden)
    grad_value_w = weight_dot(memory_flat, value_memory) + weight_dot(hidden_low, value_hidden)
    grad_rel_w = jnp.einsum(
        "kd,ske->de",
        table_low,
        grad_rel.reshape(segment_count, -1, local_width),
        preferred_element_type=jnp.float32,
    )
    grad_hidden_part = (
        back_dot(grad_query, attention_eff[0])
        + back_dot(key_hidden, attention_eff[1])
        + back_dot(value_hidden, attention_eff[2])
    )
    grad_hidden = grad_sum_one + enter_back(grad_hidden_part)
    layer_grads = (
        jnp.stack([grad_query_w, grad_key_w, grad_value_w, grad_rel_w, grad_out_proj]),
        grad_bias,
        jnp.stack([grad_up, grad_down]),
        jnp.sum(grad_inner.astype(jnp.float32), 0),
        jnp.stack(
            [
                grad_gain_one,
                grad_offset_one,
                grad_gain_two,
                grad_offset_two,
                jnp.sum(grad_sum_two, 0),
            ]
        ),
    )
    return (grad_hidden, layer_grads)


def body(
    inputs,
    targets,
    valid_mask,
    memory,
    attention_rank,
    feedforward_rank,
    attention_weight,
    attention_moment,
    attention_average,
    feedforward_weight,
    feedforward_moment,
    feedforward_average,
    embedding_weight,
    embedding_moment,
    embedding_average,
    head_bias_weight,
    head_bias_moment,
    head_bias_average,
    inner_bias_weight,
    inner_bias_moment,
    inner_bias_average,
    norm_weight,
    norm_moment,
    norm_average,
):
    layer_count = attention_weight.shape[0]
    model_width = attention_weight.shape[2]
    segment_count, segment_length = inputs.shape
    memory_length = memory.shape[2]
    key_length = memory_length + segment_length
    vocab_size = embedding_weight.shape[0]
    attention_a = expand(attention_rank < 2, model_width // attention_rank.shape[2])
    attention_b = expand(attention_rank < 3, model_width // attention_rank.shape[2])
    feedforward_a = expand(feedforward_rank < 2, model_width // feedforward_rank.shape[2])
    feedforward_b = expand(feedforward_rank < 3, model_width // feedforward_rank.shape[2])
    rows_all = segment_count * segment_length
    token_rows = inputs.reshape(rows_all)
    target_rows = targets.reshape(rows_all)
    valid_rows = valid_mask.reshape(rows_all).astype(jnp.float32)
    vocab_ids = jnp.arange(vocab_size)
    onehot_in = (token_rows[:, None] == vocab_ids[None, :]).astype(jnp.float32)
    onehot_out = (target_rows[:, None] == vocab_ids[None, :]).astype(jnp.float32)
    hidden = jnp.dot(onehot_in, embedding_weight, precision=PRECISE)
    row_index = jnp.arange(segment_length)[:, None]
    col_index = jnp.arange(key_length)[None, :]
    allowed = memory_length + row_index - col_index >= 0
    table_low = positions(key_length, model_width).astype(HALF_TYPE)
    attention_eff = (attention_weight * attention_a).astype(HALF_TYPE)
    feedforward_eff = (feedforward_weight * feedforward_a).astype(HALF_TYPE)
    saved_states = []
    memory_next = []
    for layer_idx in range(layer_count):
        hidden, saved_state = layer_forward(
            hidden,
            memory[layer_idx],
            attention_eff[layer_idx],
            head_bias_weight[layer_idx],
            feedforward_eff[layer_idx],
            inner_bias_weight[layer_idx],
            norm_weight[layer_idx],
            table_low,
            allowed,
        )
        saved_states.append(saved_state)
        memory_next.append(saved_state[0].reshape(segment_count, segment_length, model_width))
    final_low = hidden.astype(HALF_TYPE)
    embedding_low = embedding_weight.astype(HALF_TYPE)
    logit_scale = model_width ** (-0.5)
    logits = back_dot(final_low, embedding_low) * logit_scale
    row_peak = jnp.max(logits, axis=-1, keepdims=True)
    log_total = row_peak + jnp.log(jnp.sum(jnp.exp(logits - row_peak), axis=-1, keepdims=True))
    picked = jnp.sum(logits * onehot_out, axis=-1)
    ce_local = jnp.sum(valid_rows * (log_total[:, 0] - picked))
    count_local = jnp.sum(valid_rows)
    ce_total, valid_count = lax.psum((ce_local, count_local), "dp")
    softmax_rows = jnp.exp(logits - log_total)
    grad_logits = (valid_rows[:, None] * (softmax_rows - onehot_out) / valid_count).astype(
        HALF_TYPE
    )
    grad_hidden = forward_dot(grad_logits, embedding_low) * logit_scale
    grad_embedding = weight_dot(grad_logits, final_low) * logit_scale
    layer_grads = [None] * layer_count
    for layer_idx in reversed(range(layer_count)):
        grad_hidden, layer_grads[layer_idx] = layer_backward(
            grad_hidden,
            saved_states[layer_idx],
            memory[layer_idx],
            attention_eff[layer_idx],
            feedforward_eff[layer_idx],
            norm_weight[layer_idx],
            table_low,
            allowed,
        )
    grad_embedding = grad_embedding + lax.dot_general(
        onehot_in, grad_hidden, (((0,), (0,)), ((), ())), precision=PRECISE
    )
    grad_attention = jnp.stack([entry[0] for entry in layer_grads])
    grad_head_bias = jnp.stack([entry[1] for entry in layer_grads])
    grad_feedforward = jnp.stack([entry[2] for entry in layer_grads])
    grad_inner_bias = jnp.stack([entry[3] for entry in layer_grads])
    grad_norm = jnp.stack([entry[4] for entry in layer_grads])
    grad_attention, grad_feedforward, grad_head_bias, grad_inner_bias = (
        lax.psum(grad_attention.astype(jnp.bfloat16), "dp").astype(jnp.float32),
        lax.psum(grad_feedforward.astype(jnp.bfloat16), "dp").astype(jnp.float32),
        lax.psum(grad_head_bias.astype(jnp.bfloat16), "dp").astype(jnp.float32),
        lax.psum(grad_inner_bias.astype(jnp.bfloat16), "dp").astype(jnp.float32),
    )
    grad_embedding, grad_norm = (
        lax.psum(grad_embedding.astype(jnp.bfloat16), "dp").astype(jnp.float32),
        lax.psum(grad_norm.astype(jnp.bfloat16), "dp").astype(jnp.float32),
    )
    attention_coef = attention_a + WIDEN * (attention_b - attention_a)
    feedforward_coef = feedforward_a + WIDEN * (feedforward_b - feedforward_a)
    grad_attention = (
        attention_b * grad_attention + 2.0 * PENALTY * attention_weight * attention_coef
    )
    grad_feedforward = (
        feedforward_b * grad_feedforward + 2.0 * PENALTY * feedforward_weight * feedforward_coef
    )
    groups = [
        (attention_weight, attention_moment, attention_average, grad_attention),
        (feedforward_weight, feedforward_moment, feedforward_average, grad_feedforward),
        (head_bias_weight, head_bias_moment, head_bias_average, grad_head_bias),
        (inner_bias_weight, inner_bias_moment, inner_bias_average, grad_inner_bias),
        (embedding_weight, embedding_moment, embedding_average, grad_embedding),
        (norm_weight, norm_moment, norm_average, grad_norm),
    ]
    moments_next = [MOMENTUM * entry[1] + entry[3] for entry in groups]
    directions = [
        entry[3] + MOMENTUM * moment_next for entry, moment_next in zip(groups, moments_next)
    ]
    local_sums = jnp.stack(
        [jnp.sum(entry[0] * entry[0]) for entry in groups[:4]]
        + [jnp.sum(direction * direction) for direction in directions[:4]]
    )
    totals = lax.psum(local_sums, "mp")
    weight_squares = [totals[position] for position in range(4)] + [
        jnp.sum(entry[0] * entry[0]) for entry in groups[4:]
    ]
    direction_squares = [totals[4 + position] for position in range(4)] + [
        jnp.sum(direction * direction) for direction in directions[4:]
    ]
    results = []
    for position in range(6):
        weight, moment, average, grad = groups[position]
        trust_ratio = jnp.sqrt(weight_squares[position]) / jnp.sqrt(direction_squares[position])
        weight_next = weight - RATE * trust_ratio * directions[position]
        results.append(
            (weight_next, moments_next[position], AVERAGE * average + (1.0 - AVERAGE) * weight_next)
        )
    new_memory = jnp.stack(memory_next)
    return (
        ce_total,
        valid_count,
        new_memory,
        grad_attention,
        results[0][0],
        results[0][1],
        results[0][2],
        grad_feedforward,
        results[1][0],
        results[1][1],
        results[1][2],
        results[4][0],
        results[4][1],
        results[4][2],
        results[2][0],
        results[2][1],
        results[2][2],
        results[3][0],
        results[3][1],
        results[3][2],
        grad_norm,
        results[5][0],
        results[5][1],
        results[5][2],
    )


def solution(mesh):
    return jax.shard_map(
        body,
        mesh=mesh,
        in_specs=(
            P("dp", None),
            P("dp", None),
            P("dp", None),
            P(None, "dp", None, None),
            P(None, None, None, "mp"),
            P(None, None, None, "mp"),
            P(None, None, None, "mp"),
            P(None, None, None, "mp"),
            P(None, None, None, "mp"),
            P(None, None, None, "mp"),
            P(None, None, None, "mp"),
            P(None, None, None, "mp"),
            P(),
            P(),
            P(),
            P(None, None, "mp"),
            P(None, None, "mp"),
            P(None, None, "mp"),
            P(None, "mp"),
            P(None, "mp"),
            P(None, "mp"),
            P(),
            P(),
            P(),
        ),
        out_specs=(
            P(),
            P(),
            P(None, "dp", None, None),
            P(None, None, None, "mp"),
            P(None, None, None, "mp"),
            P(None, None, None, "mp"),
            P(None, None, None, "mp"),
            P(None, None, None, "mp"),
            P(None, None, None, "mp"),
            P(None, None, None, "mp"),
            P(None, None, None, "mp"),
            P(),
            P(),
            P(),
            P(None, None, "mp"),
            P(None, None, "mp"),
            P(None, None, "mp"),
            P(None, "mp"),
            P(None, "mp"),
            P(None, "mp"),
            P(),
            P(),
            P(),
            P(),
        ),
        check_vma=False,
    )
```

profile of v0, /device:TPU:1, one launch (start us, length us, event | category | flops | bytes accessed | tf_op | source)
XLA Modules:
  0.0 1872.8 jit_solution(1175026526463772850)
XLA Ops:
  36.4 144.6 %while.72 = (s32[]{:T(128)}, bf16[4,512,1,64]{1,3,2,0:T(8,128)(2,1)S(1)}, f32[4,1,512,1]{2,3,1,0:T(1,128)S(1)}, bf16[4,1024,1,64]{1,3,2,0:T(8,128)(2,1)}, bf16[4...) while((s32[]{:T(128)}, ...), condition=%wide.region_3.4_spmd.clone, body=%wide.region_0.3_spmd.clone.sunk | while | flops 206601728 | bytes 27882100 | solution.py:209
  43.1 24.2 %slice_reduce_fusion.8 = f32[524288]{0:T(1024)} fusion(f32[1,524800]{1,0:T(1,128)} %reshape.1020), kind=kLoop, calls=%fused_computation.4.clone.1 | loop fusion | bytes 4194304 | tf_op jit(solution)/shard_map/while/body/eval_jaxpr/slice | solution.py:90
  79.2 24.2 %slice_reduce_fusion.8 = f32[524288]{0:T(1024)} fusion(f32[1,524800]{1,0:T(1,128)} %reshape.1020), kind=kLoop, calls=%fused_computation.4.clone.1 | loop fusion | bytes 4194304 | tf_op jit(solution)/shard_map/while/body/eval_jaxpr/slice | solution.py:90
  115.3 24.2 %slice_reduce_fusion.8 = f32[524288]{0:T(1024)} fusion(f32[1,524800]{1,0:T(1,128)} %reshape.1020), kind=kLoop, calls=%fused_computation.4.clone.1 | loop fusion | bytes 4194304 | tf_op jit(solution)/shard_map/while/body/eval_jaxpr/slice | solution.py:90
  151.4 24.2 %slice_reduce_fusion.8 = f32[524288]{0:T(1024)} fusion(f32[1,524800]{1,0:T(1,128)} %reshape.1020), kind=kLoop, calls=%fused_computation.4.clone.1 | loop fusion | bytes 4194304 | tf_op jit(solution)/shard_map/while/body/eval_jaxpr/slice | solution.py:90
  191.2 68.5 %all-reduce.19.cloned.1.call-done = f32[2048,512]{1,0:T(8,128)} async-done(((f32[2048,512]{1,0:T(8,128)}), f32[2048,512]{1,0:T(8,128)}) %all-reduce.19.cloned.1.call-update) | async-done | bytes 4194320 | tf_op jit(solution)/shard_map/psum | solution.py:79
  281.0 63.8 %all-reduce.21.cloned.1.call-done = f32[2048,512]{1,0:T(8,128)} async-done(((f32[2048,512]{1,0:T(8,128)}), f32[2048,512]{1,0:T(8,128)}) %all-reduce.21.cloned.1.call-update) | async-done | bytes 4194320 | tf_op jit(solution)/shard_map/psum | solution.py:79
  363.5 146.6 %while.73 = (s32[]{:T(128)}, bf16[4,512,1,64]{1,3,2,0:T(8,128)(2,1)S(1)}, f32[4,1,512,1]{2,3,1,0:T(1,128)}, bf16[4,1024,1,64]{1,3,2,0:T(8,128)(2,1)}, bf16[4,512...) while((s32[]{:T(128)}, ...), condition=%wide.region_13.14_spmd.clone, body=%wide.region_10.13_spmd.clone.sunk | while | flops 206601728 | bytes 27882608 | solution.py:209
  370.1 24.2 %slice_reduce_fusion.9 = f32[524288]{0:T(1024)} fusion(f32[1,524800]{1,0:T(1,128)} %reshape.1022), kind=kLoop, calls=%fused_computation.28.clone.1 | loop fusion | bytes 4194304 | tf_op jit(solution)/shard_map/while/body/eval_jaxpr/slice | solution.py:90
  406.7 24.2 %slice_reduce_fusion.9 = f32[524288]{0:T(1024)} fusion(f32[1,524800]{1,0:T(1,128)} %reshape.1022), kind=kLoop, calls=%fused_computation.28.clone.1 | loop fusion | bytes 4194304 | tf_op jit(solution)/shard_map/while/body/eval_jaxpr/slice | solution.py:90
  443.3 24.2 %slice_reduce_fusion.9 = f32[524288]{0:T(1024)} fusion(f32[1,524800]{1,0:T(1,128)} %reshape.1022), kind=kLoop, calls=%fused_computation.28.clone.1 | loop fusion | bytes 4194304 | tf_op jit(solution)/shard_map/while/body/eval_jaxpr/slice | solution.py:90
  479.9 24.2 %slice_reduce_fusion.9 = f32[524288]{0:T(1024)} fusion(f32[1,524800]{1,0:T(1,128)} %reshape.1022), kind=kLoop, calls=%fused_computation.28.clone.1 | loop fusion | bytes 4194304 | tf_op jit(solution)/shard_map/while/body/eval_jaxpr/slice | solution.py:90
  514.1 72.6 %all-reduce.23.cloned.1.call-done = f32[2048,512]{1,0:T(8,128)} async-done(((f32[2048,512]{1,0:T(8,128)}), f32[2048,512]{1,0:T(8,128)}) %all-reduce.23.cloned.1.call-update) | async-done | bytes 4194320 | tf_op jit(solution)/shard_map/psum | solution.py:79
  600.3 71.9 %all-reduce.25.cloned.1.call-done = f32[2048,512]{1,0:T(8,128)} async-done(((f32[2048,512]{1,0:T(8,128)}), f32[2048,512]{1,0:T(8,128)}) %all-reduce.25.cloned.1.call-update) | async-done | bytes 4194320 | tf_op jit(solution)/shard_map/psum | solution.py:79
  681.7 33.9 %all-reduce.6 = (f32[]{:T(128)}, f32[]{:T(128)}) all-reduce(f32[]{:T(128)} %get-tuple-element.930, f32[]{:T(128)} %get-tuple-element.931), channel_id=1, replica_groups=mesh['dp'=16,'mp'=8] {'dp'}, use_global_device_ids=true, to_apply=%region_26.27 | all-reduce | flops 2 | bytes 16 | tf_op jit(solution)/shard_map/psum | solution.py:415
  715.7 6.1 multiply_reduce_fusion.2
  730.7 73.2 %all-reduce.27.cloned.1.call-done = f32[2048,512]{1,0:T(8,128)} async-done(((f32[2048,512]{1,0:T(8,128)}), f32[2048,512]{1,0:T(8,128)}) %all-reduce.27.cloned.1.call-update) | async-done | bytes 4194320 | tf_op jit(solution)/shard_map/psum | solution.py:83
  803.9 6.7 multiply_reduce_fusion.3
  820.9 312.7 %while.74 = (s32[]{:T(128)}, bf16[4,512,1,64]{1,3,2,0:T(8,128)(2,1)}, bf16[4,512,1,64]{1,3,2,0:T(8,128)(2,1)}, bf16[4,1024,1,64]{1,3,2,0:T(8,128)(2,1)}, bf16[4,...) while((s32[]{:T(128)}, ...), condition=%wide.region_34.35_spmd.clone, body=%wide.region_32.34_spmd.clone.sunk | while | flops 543620608 | bytes 56127672 | solution.py:288
  827.6 22.9 %slice_reduce_fusion.10 = f32[524288]{0:T(1024)S(1)} fusion(f32[1,524800]{1,0:T(1,128)} %reshape.1024), kind=kLoop, calls=%fused_computation.53.clone.1 | loop fusion | bytes 4194304 | tf_op jit(solution)/shard_map/while/body/eval_jaxpr/slice | solution.py:90
  858.1 23.0 %pad_reduce_fusion.4 = bf16[524800]{0:T(1024)(128)(2,1)} fusion(bf16[1,524288]{1,0:T(2,128)(2,1)S(1)} %bitcast.704), kind=kLoop, calls=%fused_computation.52.clone.1 | loop fusion | bytes 2098176 | tf_op jit(solution)/shard_map/while/body/eval_jaxpr/jit(_pad)/pad | solution.py:98
  905.6 22.9 %slice_reduce_fusion.10 = f32[524288]{0:T(1024)S(1)} fusion(f32[1,524800]{1,0:T(1,128)} %reshape.1024), kind=kLoop, calls=%fused_computation.53.clone.1 | loop fusion | bytes 4194304 | tf_op jit(solution)/shard_map/while/body/eval_jaxpr/slice | solution.py:90
  936.2 23.0 %pad_reduce_fusion.4 = bf16[524800]{0:T(1024)(128)(2,1)} fusion(bf16[1,524288]{1,0:T(2,128)(2,1)S(1)} %bitcast.704), kind=kLoop, calls=%fused_computation.52.clone.1 | loop fusion | bytes 2098176 | tf_op jit(solution)/shard_map/while/body/eval_jaxpr/jit(_pad)/pad | solution.py:98
  983.7 22.9 %slice_reduce_fusion.10 = f32[524288]{0:T(1024)S(1)} fusion(f32[1,524800]{1,0:T(1,128)} %reshape.1024), kind=kLoop, calls=%fused_computation.53.clone.1 | loop fusion | bytes 4194304 | tf_op jit(solution)/shard_map/while/body/eval_jaxpr/slice | solution.py:90
  1014.2 23.0 %pad_reduce_fusion.4 = bf16[524800]{0:T(1024)(128)(2,1)} fusion(bf16[1,524288]{1,0:T(2,128)(2,1)S(1)} %bitcast.704), kind=kLoop, calls=%fused_computation.52.clone.1 | loop fusion | bytes 2098176 | tf_op jit(solution)/shard_map/while/body/eval_jaxpr/jit(_pad)/pad | solution.py:98
  1061.7 22.9 %slice_reduce_fusion.10 = f32[524288]{0:T(1024)S(1)} fusion(f32[1,524800]{1,0:T(1,128)} %reshape.1024), kind=kLoop, calls=%fused_computation.53.clone.1 | loop fusion | bytes 4194304 | tf_op jit(solution)/shard_map/while/body/eval_jaxpr/slice | solution.py:90
  1092.3 23.0 %pad_reduce_fusion.4 = bf16[524800]{0:T(1024)(128)(2,1)} fusion(bf16[1,524288]{1,0:T(2,128)(2,1)S(1)} %bitcast.704), kind=kLoop, calls=%fused_computation.52.clone.1 | loop fusion | bytes 2098176 | tf_op jit(solution)/shard_map/while/body/eval_jaxpr/jit(_pad)/pad | solution.py:98
  1156.9 60.2 %all-reduce.29.cloned.1.call-done = f32[2048,512]{1,0:T(8,128)} async-done(((f32[2048,512]{1,0:T(8,128)}), f32[2048,512]{1,0:T(8,128)}) %all-reduce.29.cloned.1.call-update) | async-done | bytes 4194320 | tf_op jit(solution)/shard_map/psum | solution.py:83
  1217.1 6.8 multiply_reduce_fusion.4
  1242.2 61.7 %all-reduce.31.cloned.1.call-done = f32[2048,512]{1,0:T(8,128)} async-done(((f32[2048,512]{1,0:T(8,128)}), f32[2048,512]{1,0:T(8,128)}) %all-reduce.31.cloned.1.call-update) | async-done | bytes 4194320 | tf_op jit(solution)/shard_map/psum | solution.py:83
  1303.9 6.2 multiply_reduce_fusion.5
  1320.5 312.3 %while.75 = (s32[]{:T(128)}, bf16[4,512,1,64]{1,3,2,0:T(8,128)(2,1)}, bf16[4,512,1,64]{1,3,2,0:T(8,128)(2,1)}, bf16[4,1024,1,64]{1,3,2,0:T(8,128)(2,1)}, bf16[4,...) while((s32[]{:T(128)}, ...), condition=%wide.region_43.44_spmd.clone, body=%wide.region_41.43_spmd.clone.sunk | while | flops 543620608 | bytes 56127672 | solution.py:288
  1327.1 22.9 %slice_reduce_fusion.11 = f32[524288]{0:T(1024)S(1)} fusion(f32[1,524800]{1,0:T(1,128)} %reshape.1027), kind=kLoop, calls=%fused_computation.110.clone.1 | loop fusion | bytes 4194304 | tf_op jit(solution)/shard_map/while/body/eval_jaxpr/slice | solution.py:90
  1357.6 23.0 %pad_reduce_fusion.5 = bf16[524800]{0:T(1024)(128)(2,1)} fusion(bf16[1,524288]{1,0:T(2,128)(2,1)S(1)} %bitcast.705), kind=kLoop, calls=%fused_computation.109.clone.1 | loop fusion | bytes 2098176 | tf_op jit(solution)/shard_map/while/body/eval_jaxpr/jit(_pad)/pad | solution.py:98
  1405.1 22.9 %slice_reduce_fusion.11 = f32[524288]{0:T(1024)S(1)} fusion(f32[1,524800]{1,0:T(1,128)} %reshape.1027), kind=kLoop, calls=%fused_computation.110.clone.1 | loop fusion | bytes 4194304 | tf_op jit(solution)/shard_map/while/body/eval_jaxpr/slice | solution.py:90
  1435.6 23.0 %pad_reduce_fusion.5 = bf16[524800]{0:T(1024)(128)(2,1)} fusion(bf16[1,524288]{1,0:T(2,128)(2,1)S(1)} %bitcast.705), kind=kLoop, calls=%fused_computation.109.clone.1 | loop fusion | bytes 2098176 | tf_op jit(solution)/shard_map/while/body/eval_jaxpr/jit(_pad)/pad | solution.py:98
  1483.1 22.9 %slice_reduce_fusion.11 = f32[524288]{0:T(1024)S(1)} fusion(f32[1,524800]{1,0:T(1,128)} %reshape.1027), kind=kLoop, calls=%fused_computation.110.clone.1 | loop fusion | bytes 4194304 | tf_op jit(solution)/shard_map/while/body/eval_jaxpr/slice | solution.py:90
  1513.6 23.0 %pad_reduce_fusion.5 = bf16[524800]{0:T(1024)(128)(2,1)} fusion(bf16[1,524288]{1,0:T(2,128)(2,1)S(1)} %bitcast.705), kind=kLoop, calls=%fused_computation.109.clone.1 | loop fusion | bytes 2098176 | tf_op jit(solution)/shard_map/while/body/eval_jaxpr/jit(_pad)/pad | solution.py:98
  1561.1 22.9 %slice_reduce_fusion.11 = f32[524288]{0:T(1024)S(1)} fusion(f32[1,524800]{1,0:T(1,128)} %reshape.1027), kind=kLoop, calls=%fused_computation.110.clone.1 | loop fusion | bytes 4194304 | tf_op jit(solution)/shard_map/while/body/eval_jaxpr/slice | solution.py:90
  1591.6 23.0 %pad_reduce_fusion.5 = bf16[524800]{0:T(1024)(128)(2,1)} fusion(bf16[1,524288]{1,0:T(2,128)(2,1)S(1)} %bitcast.705), kind=kLoop, calls=%fused_computation.109.clone.1 | loop fusion | bytes 2098176 | tf_op jit(solution)/shard_map/while/body/eval_jaxpr/jit(_pad)/pad | solution.py:98
  1653.6 62.7 %all-reduce.33.cloned.1.call-done = f32[2048,512]{1,0:T(8,128)} async-done(((f32[2048,512]{1,0:T(8,128)}), f32[2048,512]{1,0:T(8,128)}) %all-reduce.33.cloned.1.call-update) | async-done | bytes 4194320 | tf_op jit(solution)/shard_map/psum | solution.py:83
  1716.2 6.4 fusion.122
  1734.0 61.3 %all-reduce.7 = (bf16[2,5,512]{2,1,0:T(8,128)(2,1)S(1)}, bf16[2,2,64]{2,1,0:T(2,128)(2,1)S(1)}, bf16[2,256]{1,0:T(2,128)(2,1)S(1)}) all-reduce(bf16[2,5,512]{2,1,0:T(8,128)(2,1)S(1)} %pad_maximum_fusion.4, bf16[2,2,64]{2,1,0:T(2,128)(2,1)S(1)} %pad_maximum_fusion.5, ...), channel_id=1, replica_groups=mesh['dp'=16,'mp'=8] {'dp'}, use_global_device_ids=true, to_apply=%region_79.80 | all-reduce | flops 5888 | bytes 23552 | tf_op jit(solution)/shard_map/psum | solution.py:450
  1799.8 15.9 all-reduce.35.cloned.1.call-done
  1815.7 7.2 multiply_reduce_fusion.19
  1825.5 5.2 stack.279
  1831.4 13.5 psum.132
  1858.6 5.2 multiply_add_fusion.7
  (733 shorter events, 576.5 us)
Async XLA Ops:
  7.2 252.5 %all-reduce.19.cloned.1.call-start = ((), (), s32[]{:S(2)}) async-start(), calls=%async_computation | async-start | bytes 8388608 | tf_op jit(solution)/shard_map/psum | solution.py:79
  11.0 9.5 copy-start.52
  14.5 11.2 copy-start.8
  28.2 7.2 copy-start.73
  185.6 159.1 %all-reduce.21.cloned.1.call-start = ((), (), s32[]{:S(2)}) async-start(), calls=%async_computation.1 | async-start | bytes 8388608 | tf_op jit(solution)/shard_map/psum | solution.py:79
  189.8 73.9 %copy-start.55 = (pred[2,2,512,256]{3,2,1,0:T(8,128)(4,1)}, pred[2,2,512,256]{3,2,1,0:T(8,128)(4,1)S(1)}, u32[]{:S(2)}) copy-start(pred[2,2,512,256]{3,2,1,0:T(8,128)(4,1)S(1)} %copy.125) | copy-start | bytes 1572868
  189.9 154.8 %copy-start.95 = (f32[1,1,512]{2,0,1:T(1,128)}, f32[1,1,512]{2,0,1:T(1,128)S(1)}, u32[]{:S(2)}) copy-start(f32[1,1,512]{2,0,1:T(1,128)S(1)} %get-tuple-element.1108) | copy-start | bytes 6148
  263.7 81.0 %copy-start.81 = (f32[2048]{0:T(1024)}, f32[2048]{0:T(1024)S(1)}, u32[]{:S(2)}) copy-start(f32[2048]{0:T(1024)S(1)} %broadcast_multiply_fusion.11) | copy-start | bytes 24580
  264.6 80.1 %copy-start.85 = (f32[2048]{0:T(1024)}, f32[2048]{0:T(1024)S(1)}, u32[]{:S(2)}) copy-start(f32[2048]{0:T(1024)S(1)} %add_rsqrt_fusion.3) | copy-start | bytes 24580
  272.0 314.8 %all-reduce.23.cloned.1.call-start = ((), (), s32[]{:S(2)}) async-start(), calls=%async_computation.2 | async-start | bytes 8388608 | tf_op jit(solution)/shard_map/psum | solution.py:79
  349.8 237.0 %copy-start.83 = (f32[2048]{0:T(1024)}, f32[2048]{0:T(1024)S(1)}, u32[]{:S(2)}) copy-start(f32[2048]{0:T(1024)S(1)} %add_rsqrt_fusion.2) | copy-start | bytes 24580
  514.1 158.1 %all-reduce.25.cloned.1.call-start = ((), (), s32[]{:S(2)}) async-start(), calls=%async_computation.3 | async-start | bytes 8388608 | tf_op jit(solution)/shard_map/psum | solution.py:79
  599.5 204.3 %all-reduce.27.cloned.1.call-start = ((), (), s32[]{:S(2)}) async-start(), calls=%async_computation.4 | async-start | bytes 8388608 | tf_op jit(solution)/shard_map/psum | solution.py:83
  600.2 115.4 %copy-start.98 = (s32[1,4,4,128]{3,1,2,0:T(4,128)}, s32[1,4,4,128]{3,1,2,0:T(4,128)S(1)}, u32[]{:S(2)}) copy-start(s32[1,4,4,128]{3,1,2,0:T(4,128)S(1)} %copy.173) | copy-start | bytes 24580
  600.2 115.4 %copy-start.111 = (f32[1,4,4,128]{3,1,2,0:T(4,128)}, f32[1,4,4,128]{3,1,2,0:T(4,128)S(1)}, u32[]{:S(2)}) copy-start(f32[1,4,4,128]{3,1,2,0:T(4,128)S(1)} %copy.174) | copy-start | bytes 24580
  680.5 41.2 %copy-start.33 = (f32[2048,256]{0,1:T(8,128)}, f32[2048,256]{0,1:T(8,128)S(1)}, u32[]{:S(2)}) copy-start(f32[2048,256]{0,1:T(8,128)S(1)} %get-tuple-element.1132) | copy-start | bytes 6291460
  681.1 40.7 %copy-start.107 = (f32[2048]{0:T(1024)}, f32[2048]{0:T(1024)S(1)}, u32[]{:S(2)}) copy-start(f32[2048]{0:T(1024)S(1)} %get-tuple-element.1064) | copy-start | bytes 24580
  730.6 486.5 %all-reduce.29.cloned.1.call-start = ((), (), s32[]{:S(2)}) async-start(), calls=%async_computation.5 | async-start | bytes 8388608 | tf_op jit(solution)/shard_map/psum | solution.py:83
  803.9 6.7 copy-start.5
  1144.4 159.5 %all-reduce.31.cloned.1.call-start = ((), (), s32[]{:S(2)}) async-start(), calls=%async_computation.6 | async-start | bytes 8388608 | tf_op jit(solution)/shard_map/psum | solution.py:83
  1155.3 61.8 %copy-start.84 = (f32[2048]{0:T(1024)S(1)}, f32[2048]{0:T(1024)}, u32[]{:S(2)}) copy-start(f32[2048]{0:T(1024)} %copy-done.83) | copy-start | bytes 24580
  1217.1 6.8 copy-start.3
  1231.2 485.0 %all-reduce.33.cloned.1.call-start = ((), (), s32[]{:S(2)}) async-start(), calls=%async_computation.7 | async-start | bytes 8388608 | tf_op jit(solution)/shard_map/psum | solution.py:83
  1231.3 8.2 copy-start.37
  1241.1 62.9 %copy-start.82 = (f32[2048]{0:T(1024)S(1)}, f32[2048]{0:T(1024)}, u32[]{:S(2)}) copy-start(f32[2048]{0:T(1024)} %copy-done.81) | copy-start | bytes 24580
  1241.1 62.8 %copy-start.86 = (f32[2048]{0:T(1024)S(1)}, f32[2048]{0:T(1024)}, u32[]{:S(2)}) copy-start(f32[2048]{0:T(1024)} %copy-done.85) | copy-start | bytes 24580
  1241.1 62.8 %copy-start.96 = (f32[1,1,512]{2,0,1:T(1,128)S(1)}, f32[1,1,512]{2,0,1:T(1,128)}, u32[]{:S(2)}) copy-start(f32[1,1,512]{2,0,1:T(1,128)} %copy-done.95) | copy-start | bytes 6148
  1643.5 172.1 %all-reduce.35.cloned.1.call-start = ((), (), s32[]{:S(2)}) async-start(), calls=%async_computation.8 | async-start | bytes 3932160 | tf_op jit(solution)/shard_map/psum | solution.py:443
  1651.2 65.0 %copy-start.92 = (s32[1,4,4,128]{3,1,2,0:T(4,128)S(1)}, s32[1,4,4,128]{3,1,2,0:T(4,128)}, u32[]{:S(2)}) copy-start(s32[1,4,4,128]{3,1,2,0:T(4,128)} %copy-done.91) | copy-start | bytes 24580
  1653.5 69.1 %copy-start.99 = (s32[1,4,4,128]{3,1,2,0:T(4,128)S(1)}, s32[1,4,4,128]{3,1,2,0:T(4,128)}, u32[]{:S(2)}) copy-start(s32[1,4,4,128]{3,1,2,0:T(4,128)} %copy-done.98) | copy-start | bytes 24580
  1653.5 69.1 %copy-start.108 = (f32[2048]{0:T(1024)S(1)}, f32[2048]{0:T(1024)}, u32[]{:S(2)}) copy-start(f32[2048]{0:T(1024)} %copy-done.107) | copy-start | bytes 24580
  1653.5 69.1 %copy-start.112 = (f32[1,4,4,128]{3,1,2,0:T(4,128)S(1)}, f32[1,4,4,128]{3,1,2,0:T(4,128)}, u32[]{:S(2)}) copy-start(f32[1,4,4,128]{3,1,2,0:T(4,128)} %copy-done.111) | copy-start | bytes 24580
  1716.2 6.5 copy-start.42
  1728.9 67.0 %copy-start.90 = (f32[2,5,512]{2,0,1:T(2,128)S(1)}, f32[2,5,512]{2,0,1:T(2,128)}, u32[]{:S(2)}) copy-start(f32[2,5,512]{2,0,1:T(2,128)} %param.54) | copy-start | bytes 61444
  1728.9 68.3 %copy-start.89 = (f32[2,5,512]{2,0,1:T(2,128)S(1)}, f32[2,5,512]{2,0,1:T(2,128)}, u32[]{:S(2)}) copy-start(f32[2,5,512]{2,0,1:T(2,128)} %param.53) | copy-start | bytes 61444
  1728.9 68.3 %copy-start.101 = (f32[2,5,512]{2,0,1:T(2,128)S(1)}, f32[2,5,512]{2,0,1:T(2,128)}, u32[]{:S(2)}) copy-start(f32[2,5,512]{2,0,1:T(2,128)} %param.55) | copy-start | bytes 61444
  1729.0 69.6 %copy-start.125 = (f32[2,2,64]{2,1,0:T(2,128)S(1)}, f32[2,2,64]{2,1,0:T(2,128)}, u32[]{:S(2)}) copy-start(f32[2,2,64]{2,1,0:T(2,128)} %param.48) | copy-start | bytes 3076
  1729.0 70.2 %copy-start.126 = (f32[2,256]{1,0:T(2,128)S(1)}, f32[2,256]{1,0:T(2,128)}, u32[]{:S(2)}) copy-start(f32[2,256]{1,0:T(2,128)} %param.51) | copy-start | bytes 6148
  1799.2 56.2 %copy-start.115 = (f32[2,2,64]{2,1,0:T(2,128)}, f32[2,2,64]{2,1,0:T(2,128)S(1)}, u32[]{:S(2)}) copy-start(f32[2,2,64]{2,1,0:T(2,128)S(1)} %get-tuple-element.1049) | copy-start | bytes 3076
  1799.8 55.0 %copy-start.116 = (f32[2,256]{1,0:T(2,128)}, f32[2,256]{1,0:T(2,128)S(1)}, u32[]{:S(2)}) copy-start(f32[2,256]{1,0:T(2,128)S(1)} %get-tuple-element.1047) | copy-start | bytes 6148
  1815.7 7.2 copy-start.43
  1815.7 7.2 copy-start.69
  1815.7 7.2 copy-start.75
  1822.9 31.8 %copy-start.127 = (f32[2,256]{1,0:T(2,128)S(1)}, f32[2,256]{1,0:T(2,128)}, u32[]{:S(2)}) copy-start(f32[2,256]{1,0:T(2,128)} %param.52) | copy-start | bytes 6148
  1822.9 32.4 %copy-start.106 = (f32[2,2,64]{2,1,0:T(2,128)S(1)}, f32[2,2,64]{2,1,0:T(2,128)}, u32[]{:S(2)}) copy-start(f32[2,2,64]{2,1,0:T(2,128)} %param.47) | copy-start | bytes 3076
  1822.9 32.4 %copy-start.128 = (f32[2,2,64]{2,1,0:T(2,128)S(1)}, f32[2,2,64]{2,1,0:T(2,128)}, u32[]{:S(2)}) copy-start(f32[2,2,64]{2,1,0:T(2,128)} %param.49) | copy-start | bytes 3076
  1848.3 10.2 copy-start.27
  1851.8 6.7 copy-start.44
  (99 other events, 291.6 us)
Sparse Core Ops, SparseCore 0:
  185.7 73.9 all-reduce.18
  272.1 72.5 all-reduce.20
  514.2 72.5 all-reduce.22
  599.7 72.4 all-reduce.24
  730.7 73.0 all-reduce.26
  1144.5 72.5 all-reduce.28
  1231.3 72.5 all-reduce.30
  1643.7 72.5 all-reduce.32
  1725.0 90.6 all-reduce.34
where the time goes:
time: 1880 us; the launch traced here: 1870 us
  local copies, waits for them, and re-layouts  821 us (44%)
  waiting for transfers between devices  551 us (29%)
  matrix products  247 us (13%)
  other arithmetic  118 us (6%)
  blocking collectives  109 us (6%)
  between operations  24.5 us (1%)
    slice x16, local copies, waits for them, and re-layouts, skew_rows(): flat[:, query_count - 1:query_count - 1 + query_count * key_count]  377 us
    psum x4, waiting for transfers between devices, leave_rows(): return lax.psum(partial_value, 'mp')  277 us
    psum x4, waiting for transfers between devices, enter_back(): return lax.psum(partial_value, 'mp')  258 us
    pad x8, local copies, waits for them, and re-layouts, unskew_rows(): padded = jnp.pad(flat, ((0, 0), (query_count - 1, 1)))  184 us
    reshape x16, local copies, waits for them, and re-layouts, skew_rows(): flat = padded.reshape(heads_here, query_count * (key_count + 1))  79.6 us
    psum x1, blocking collectives, body(): lax.psum(grad_norm.astype(jnp.bfloat16), 'dp').astype(jnp.float32)  61.3 us
    unnamed x285, local copies, waits for them, and re-layouts  39.9 us
  transfers between devices with their start and end apart: 9, of which 9 were waited for; matrix products, arithmetic and copies ran while one was open for 3% of the time, Pallas kernels for 0%

commit v1 on v0

v1 whole, which is shorter than its diff:
```python
import functools

import jax
import jax.numpy as jnp
import numpy as np
from jax import lax
from jax.experimental import pallas as pl
from jax.experimental.pallas import tpu as pltpu
from jax.sharding import PartitionSpec as P

HD = 64
D = 512
FF = 2048
SEG = 512
KLEN = 1024
OWN = 256
HEADS = 8
VOCAB = 256
MP = 8

EPSILON = 1e-05
MOMENTUM = 0.9
AVERAGE = 0.9
RATE = 0.3
PENALTY = 0.0001
WIDEN = 5.0
F32 = jnp.float32
BF16 = jnp.bfloat16
SCALE = HD ** (-0.5)


def dot_nn(a, b):
    return lax.dot_general(a, b, (((1,), (0,)), ((), ())), preferred_element_type=F32)


def dot_nt(a, b):
    return lax.dot_general(a, b, (((1,), (1,)), ((), ())), preferred_element_type=F32)


def smooth_unit(v):
    return 0.5 * v * (1.0 + jnp.tanh(0.7978845608028654 * (v + 0.044715 * v * v * v)))


def smooth_both(v):
    squared = v * v
    t = jnp.tanh(0.7978845608028654 * (v + 0.044715 * squared * v))
    half = 0.5 * (1.0 + t)
    slope = half + 0.5 * v * (1.0 - t * t) * (
        0.7978845608028654 * (1.0 + 3.0 * 0.044715 * squared)
    )
    return v * half, slope


def tables():
    freq = (1.0 / 10000.0 ** (np.arange(0, D, 2).astype(np.float32) / np.float32(D))).astype(
        np.float32
    )
    turned = []
    for half in range(2):
        distance = (SEG + half * OWN - np.arange(KLEN)) % KLEN
        angle = (distance.astype(np.float32)[:, None] * freq[None, :]).astype(np.float64)
        turned.append(np.concatenate([np.sin(angle), np.cos(angle)], axis=1).astype(np.float32))
    return jnp.asarray(np.stack(turned), BF16)


def norm_forward(values):
    centred = values - jnp.mean(values, axis=-1, keepdims=True)
    inverse = lax.rsqrt(jnp.mean(centred * centred, axis=-1, keepdims=True) + EPSILON)
    return centred * inverse, inverse


def norm_backward(grad, normed, inverse, gain):
    scaled = grad * gain
    grad_in = inverse * (
        scaled
        - jnp.mean(scaled, axis=-1, keepdims=True)
        - normed * jnp.mean(scaled * normed, axis=-1, keepdims=True)
    )
    return (
        grad_in,
        jnp.sum(grad * normed, axis=0, keepdims=True),
        jnp.sum(grad, axis=0, keepdims=True),
    )


def transposed(value):
    return value.astype(F32).T


def forward_kernel(
    offset_ref,
    hidden_ref,
    low_ref,
    memory_ref,
    att_ref,
    ff_ref,
    bias_ref,
    inner_bias_ref,
    norm_ref,
    table_ref,
    out_ref,
    prob_ref,
    query_u_ref,
    query_w_ref,
    mixed_ref,
    normed_one_ref,
    inverse_one_ref,
    normed_two_ref,
    inverse_two_ref,
    keys_ref,
    values_ref,
    rel_ref,
    score_ref,
    low_prob_ref,
    part_ref,
):
    own_low = hidden_ref[...].astype(BF16)
    query = dot_nt(own_low, att_ref[0])
    query_u_ref[...] = (query + bias_ref[0:1, :]).astype(BF16)
    query_w_ref[...] = (query + bias_ref[1:2, :]).astype(BF16)
    for half, source in ((0, memory_ref), (1, low_ref)):
        rows = source[...]
        cols = slice(half * SEG, (half + 1) * SEG)
        keys_ref[:, cols] = dot_nt(att_ref[1], rows).astype(BF16)
        values = dot_nt(rows, att_ref[2]).astype(BF16)
        values_ref[0, cols, :] = values[:, 0:256]
        values_ref[1, cols, :] = values[:, 256:512]
    rel_ref[...] = dot_nt(att_ref[3], table_ref[...]).astype(BF16)
    offset = offset_ref[0]
    lane_head = lax.broadcasted_iota(jnp.int32, (OWN, 256), 1) // HD
    part_ref[...] = jnp.zeros_like(part_ref)

    def head(h, carry):
        group = h // 4
        mine = lane_head == h % 4
        lanes = pl.ds(pl.multiple_of(group * 256, 256), 256)
        query_u = jnp.where(mine, query_u_ref[:, lanes].astype(F32), 0.0).astype(BF16)
        query_w = jnp.where(mine, query_w_ref[:, lanes].astype(F32), 0.0).astype(BF16)
        score_ref[...] = dot_nn(query_w, rel_ref[lanes, :])
        prob_ref[h] = dot_nn(query_u, keys_ref[lanes, :])
        for b in range(0, OWN, ROWS):
            rows = slice(b, b + ROWS)
            moved = pltpu.roll(score_ref[rows, :], b, 1, stride=1, stride_axis=0)
            score = (prob_ref[h, rows, :] + moved) * SCALE
            key_id = lax.broadcasted_iota(jnp.int32, (ROWS, KLEN), 1)
            query_id = lax.broadcasted_iota(jnp.int32, (ROWS, KLEN), 0) + (offset + b + SEG)
            score = jnp.where(key_id <= query_id, score, -1e30)
            expo = jnp.exp(score - jnp.max(score, axis=-1, keepdims=True))
            prob = expo * (1.0 / jnp.sum(expo, axis=-1, keepdims=True))
            prob_ref[h, rows, :] = prob
            low_prob_ref[rows, :] = prob.astype(BF16)
        mixed = dot_nn(low_prob_ref[...], values_ref[group])
        part_ref[group] = part_ref[group] + jnp.where(mine, mixed, 0.0)
        return carry

    lax.fori_loop(0, HEADS, head, 0)
    mixed_ref[:, 0:256] = part_ref[0].astype(BF16)
    mixed_ref[:, 256:512] = part_ref[1].astype(BF16)
    attended = dot_nn(mixed_ref[...], att_ref[4])
    normed_one, inverse_one = norm_forward(hidden_ref[...] + attended)
    normed_one_ref[...] = normed_one
    inverse_one_ref[...] = inverse_one
    middle = normed_one * norm_ref[0:1, :] + norm_ref[1:2, :]
    middle_low = middle.astype(BF16)

    def units(m, branch):
        inner = dot_nn(middle_low, ff_ref[0, m]) + inner_bias_ref[m]
        return branch + dot_nt(smooth_unit(inner).astype(BF16), ff_ref[1, m])

    branch = lax.fori_loop(0, MP, units, jnp.zeros((OWN, D), F32))
    normed_two, inverse_two = norm_forward(middle + (branch + norm_ref[4:5, :]))
    normed_two_ref[...] = normed_two
    inverse_two_ref[...] = inverse_two
    out_ref[...] = normed_two * norm_ref[2:3, :] + norm_ref[3:4, :]


ROWS = 64
VMEM_SPEC = pl.BlockSpec(memory_space=pltpu.VMEM)
SMEM_SPEC = pl.BlockSpec(memory_space=pltpu.SMEM)
VMEM_LIMIT = 60 * 1024 * 1024


def layer_forward(offset, hidden, low, memory, att, ff, bias, inner_bias, norms, table):
    shapes = [
        ((OWN, D), F32),
        ((HEADS, OWN, KLEN), F32),
        ((OWN, D), BF16),
        ((OWN, D), BF16),
        ((OWN, D), BF16),
        ((OWN, D), F32),
        ((OWN, 1), F32),
        ((OWN, D), F32),
        ((OWN, 1), F32),
    ]
    return pl.pallas_call(
        forward_kernel,
        out_shape=[jax.ShapeDtypeStruct(s, t) for s, t in shapes],
        in_specs=[SMEM_SPEC] + [VMEM_SPEC] * 9,
        out_specs=[VMEM_SPEC] * len(shapes),
        scratch_shapes=[
            pltpu.VMEM((D, KLEN), BF16),
            pltpu.VMEM((2, KLEN, 256), BF16),
            pltpu.VMEM((D, KLEN), BF16),
            pltpu.VMEM((OWN, KLEN), F32),
            pltpu.VMEM((OWN, KLEN), BF16),
            pltpu.VMEM((2, OWN, 256), F32),
        ],
        compiler_params=pltpu.CompilerParams(vmem_limit_bytes=VMEM_LIMIT),
        name="layer_forward",
    )(offset, hidden, low, memory, att, ff, bias, inner_bias, norms, table)


def backward_kernel(
    offset_ref,
    grad_ref,
    hidden_ref,
    low_ref,
    memory_ref,
    att_ref,
    ff_ref,
    inner_bias_ref,
    norm_ref,
    table_ref,
    prob_ref,
    query_u_ref,
    query_w_ref,
    mixed_ref,
    normed_one_ref,
    inverse_one_ref,
    normed_two_ref,
    inverse_two_ref,
    grad_own_ref,
    kept_ref,
    sent_ref,
    grad_att_ref,
    grad_kv_ref,
    grad_ff_ref,
    grad_bias_ref,
    grad_inner_bias_ref,
    grad_norm_ref,
    keys_ref,
    values_ref,
    rel_ref,
    gmix_ref,
    gmix_t_ref,
    query_t_ref,
    flip_t_ref,
    prob_grad_ref,
    score_grad_ref,
    low_prob_ref,
    turned_ref,
    gquery_ref,
    gkv_ref,
    grel_ref,
):
    own_low = hidden_ref[...].astype(BF16)
    gsum_two, ggain_two, goffset_two = norm_backward(
        grad_ref[...], normed_two_ref[...], inverse_two_ref[...], norm_ref[2:3, :]
    )
    middle = normed_one_ref[...] * norm_ref[0:1, :] + norm_ref[1:2, :]
    middle_low = middle.astype(BF16)
    middle_t = transposed(middle_low).astype(BF16)
    gbranch = gsum_two.astype(BF16)
    gbranch_t = transposed(gbranch).astype(BF16)

    def units(m, gmiddle):
        inner = dot_nn(middle_low, ff_ref[0, m]) + inner_bias_ref[m]
        active, slope = smooth_both(inner)
        ginner = (dot_nn(gbranch, ff_ref[1, m]) * slope).astype(BF16)
        grad_ff_ref[0, m] = dot_nn(middle_t, ginner).astype(BF16)
        grad_ff_ref[1, m] = dot_nn(gbranch_t, active.astype(BF16)).astype(BF16)
        grad_inner_bias_ref[m] = jnp.sum(ginner.astype(F32), axis=0, keepdims=True)
        return gmiddle + dot_nt(ginner, ff_ref[0, m])

    gmiddle = lax.fori_loop(0, MP, units, gsum_two)
    gsum_one, ggain_one, goffset_one = norm_backward(
        gmiddle, normed_one_ref[...], inverse_one_ref[...], norm_ref[0:1, :]
    )
    grad_norm_ref[0:1, :] = ggain_one
    grad_norm_ref[1:2, :] = goffset_one
    grad_norm_ref[2:3, :] = ggain_two
    grad_norm_ref[3:4, :] = goffset_two
    grad_norm_ref[4:5, :] = jnp.sum(gsum_two, axis=0, keepdims=True)
    grad_norm_ref[5:8, :] = jnp.zeros((3, D), F32)
    grad_own_ref[...] = gsum_one
    gattended = gsum_one.astype(BF16)
    grad_att_ref[4] = dot_nn(transposed(mixed_ref[...]).astype(BF16), gattended).astype(BF16)
    gmix = dot_nt(gattended, att_ref[4])
    gmix_ref[...] = gmix.astype(BF16)
    gmix_t_ref[...] = gmix.T.astype(BF16)
    query_t_ref[...] = transposed(query_u_ref[...]).astype(BF16)
    flip = (
        lax.broadcasted_iota(jnp.int32, (OWN, OWN), 0)
        + lax.broadcasted_iota(jnp.int32, (OWN, OWN), 1)
        == OWN - 1
    )
    flip = jnp.where(flip, 1.0, 0.0).astype(BF16)
    flip_t_ref[...] = dot_nn(transposed(query_w_ref[...]).astype(BF16), flip).astype(BF16)
    for half, source in ((0, memory_ref), (1, low_ref)):
        rows = source[...]
        cols = slice(half * SEG, (half + 1) * SEG)
        values_ref[:, cols] = dot_nt(att_ref[2], rows).astype(BF16)
        keys = dot_nt(rows, att_ref[1]).astype(BF16)
        keys_ref[0, cols, :] = keys[:, 0:256]
        keys_ref[1, cols, :] = keys[:, 256:512]
    rel = dot_nt(table_ref[...], att_ref[3]).astype(BF16)
    rel_ref[0] = rel[:, 0:256]
    rel_ref[1] = rel[:, 256:512]
    gquery_ref[...] = jnp.zeros_like(gquery_ref)
    lane_head = lax.broadcasted_iota(jnp.int32, (OWN, 256), 1) // HD

    def head(h, carry):
        group = h // 4
        mine = lane_head == h % 4
        lanes = pl.ds(pl.multiple_of(group * 256, 256), 256)
        row = pl.ds(pl.multiple_of(h * HD, HD), HD)
        gmix_h = jnp.where(mine, gmix_ref[:, lanes].astype(F32), 0.0).astype(BF16)
        prob_grad_ref[...] = dot_nn(gmix_h, values_ref[lanes, :])
        for b in range(0, OWN, ROWS):
            rows = slice(b, b + ROWS)
            prob = prob_ref[h, rows, :]
            gprob = prob_grad_ref[rows, :]
            inner = jnp.sum(prob * gprob, axis=-1, keepdims=True)
            score_grad_ref[rows, :] = (prob * (gprob - inner)).astype(BF16)
            low_prob_ref[rows, :] = prob.astype(BF16)
        sgrad = score_grad_ref[...]
        gquery_ref[0, group] = gquery_ref[0, group] + jnp.where(
            mine, dot_nn(sgrad, keys_ref[group]), 0.0
        )
        gkv_ref[0, row, :] = dot_nn(query_t_ref[row, :], sgrad) * SCALE
        gkv_ref[1, row, :] = dot_nn(gmix_t_ref[row, :], low_prob_ref[...])
        flipped = dot_nn(flip, sgrad).astype(BF16)
        turned_ref[...] = pltpu.roll(flipped, KLEN - OWN + 1, 1, stride=1, stride_axis=0)
        gquery_ref[1, group] = gquery_ref[1, group] + jnp.where(
            mine, dot_nn(turned_ref[...], rel_ref[group]), 0.0
        )
        grel_ref[row, :] = (dot_nn(flip_t_ref[row, :], turned_ref[...]) * SCALE).astype(BF16)
        return carry

    lax.fori_loop(0, HEADS, head, 0)
    for group in range(2):
        lanes = slice(group * 256, (group + 1) * 256)
        gquery_u = (gquery_ref[0, group] * SCALE).astype(BF16)
        gquery_w = dot_nn(flip, (gquery_ref[1, group] * SCALE).astype(BF16))
        grad_bias_ref[0:1, lanes] = jnp.sum(gquery_u.astype(F32), axis=0, keepdims=True)
        grad_bias_ref[1:2, lanes] = jnp.sum(gquery_w, axis=0, keepdims=True)
        gquery = gquery_u.astype(F32) + gquery_w
        grad_att_ref[0, lanes, :] = dot_nn(gquery.T.astype(BF16), own_low).astype(BF16)
        grad_own_ref[...] += dot_nn(gquery.astype(BF16), att_ref[0, lanes, :])
    grad_att_ref[3] = dot_nn(grel_ref[...], table_ref[...]).astype(BF16)
    mine_at = pl.ds(pl.multiple_of(SEG + offset_ref[0], OWN), OWN)
    theirs_at = pl.ds(pl.multiple_of(SEG + OWN - offset_ref[0], OWN), OWN)
    for index in range(2):
        grad_kv_ref[index] = dot_nn(gkv_ref[index, :, 0:SEG].astype(BF16), memory_ref[...])
        kept_ref[index] = gkv_ref[index, :, mine_at]
        sent_ref[index] = gkv_ref[index, :, theirs_at]


def layer_backward(
    offset, grad, hidden, low, memory, att, ff, inner_bias, norms, table, saved
):
    shapes = [
        ((OWN, D), F32),
        ((2, D, OWN), F32),
        ((2, D, OWN), F32),
        ((5, D, D), BF16),
        ((2, D, D), F32),
        ((2, MP, D, 256), BF16),
        ((2, D), F32),
        ((MP, 1, 256), F32),
        ((8, D), F32),
    ]
    return pl.pallas_call(
        backward_kernel,
        out_shape=[jax.ShapeDtypeStruct(s, t) for s, t in shapes],
        in_specs=[SMEM_SPEC] + [VMEM_SPEC] * 17,
        out_specs=[VMEM_SPEC] * len(shapes),
        scratch_shapes=[
            pltpu.VMEM((2, KLEN, 256), BF16),
            pltpu.VMEM((D, KLEN), BF16),
            pltpu.VMEM((2, KLEN, 256), BF16),
            pltpu.VMEM((OWN, D), BF16),
            pltpu.VMEM((D, OWN), BF16),
            pltpu.VMEM((D, OWN), BF16),
            pltpu.VMEM((D, OWN), BF16),
            pltpu.VMEM((OWN, KLEN), F32),
            pltpu.VMEM((OWN, KLEN), BF16),
            pltpu.VMEM((OWN, KLEN), BF16),
            pltpu.VMEM((OWN, KLEN), BF16),
            pltpu.VMEM((2, 2, OWN, 256), F32),
            pltpu.VMEM((2, D, KLEN), F32),
            pltpu.VMEM((D, KLEN), BF16),
        ],
        compiler_params=pltpu.CompilerParams(vmem_limit_bytes=VMEM_LIMIT),
        name="layer_backward",
    )(offset, grad, hidden, low, memory, att, ff, inner_bias, norms, table, *saved)


def finish_kernel(
    grad_own_ref, kept_ref, got_ref, hidden_ref, att_ref, grad_kv_ref, grad_ref, out_ref
):
    own_low = hidden_ref[...].astype(BF16)
    grad = grad_own_ref[...]
    for index in range(2):
        total = (kept_ref[index] + got_ref[index]).astype(BF16)
        out_ref[index] = (grad_kv_ref[index] + dot_nn(total, own_low)).astype(BF16)
        grad = grad + dot_nn(transposed(total).astype(BF16), att_ref[1 + index])
    grad_ref[...] = grad


def layer_finish(grad_own, kept, got, hidden, att, grad_kv):
    return pl.pallas_call(
        finish_kernel,
        out_shape=[
            jax.ShapeDtypeStruct((OWN, D), F32),
            jax.ShapeDtypeStruct((2, D, D), BF16),
        ],
        in_specs=[VMEM_SPEC] * 6,
        out_specs=[VMEM_SPEC] * 2,
        compiler_params=pltpu.CompilerParams(vmem_limit_bytes=VMEM_LIMIT),
        name="layer_finish",
    )(grad_own, kept, got, hidden, att, grad_kv)


def expand(block_rank, block_size):
    return jnp.repeat(jnp.repeat(block_rank, block_size, axis=-2), block_size, axis=-1).astype(F32)


def ring(shift):
    return [(y * 2 + c, ((y + shift) % 4) * 2 + c) for y in range(4) for c in range(2)]


PAIR = [(i, i ^ 1) for i in range(MP)]


def gather_mp(value, place, core):
    here = jnp.stack([value] + [lax.ppermute(value, "mp", ring(s)) for s in (1, 2, 3)])
    there = lax.ppermute(here, "mp", PAIR)
    even = jnp.where(core == 0, here, there)
    odd = jnp.where(core == 0, there, here)
    both = jnp.stack([even, odd], axis=1)
    turned = jnp.concatenate([both[::-1], both[:0:-1]])
    return lax.dynamic_slice_in_dim(turned, 3 - place, 4, 0).reshape((MP,) + value.shape)


def scatter_mp(value, place, core):
    shaped = value.reshape((4, 2) + value.shape[1:])
    mine = lax.dynamic_index_in_dim(shaped, core, 1, False)
    theirs = lax.dynamic_index_in_dim(shaped, 1 - core, 1, False)
    both = mine.astype(F32) + lax.ppermute(theirs, "mp", PAIR).astype(F32)
    total = lax.dynamic_index_in_dim(both, place, 0, False)
    low = both.astype(BF16)
    for s in (1, 2, 3):
        part = lax.dynamic_index_in_dim(low, (place + s) % 4, 0, False)
        total = total + lax.ppermute(part, "mp", ring(s)).astype(F32)
    return total


def body(
    inputs,
    targets,
    valid_mask,
    memory,
    attention_rank,
    feedforward_rank,
    attention_weight,
    attention_moment,
    attention_average,
    feedforward_weight,
    feedforward_moment,
    feedforward_average,
    embedding_weight,
    embedding_moment,
    embedding_average,
    head_bias_weight,
    head_bias_moment,
    head_bias_average,
    inner_bias_weight,
    inner_bias_moment,
    inner_bias_average,
    norm_weight,
    norm_moment,
    norm_average,
):
    layers = attention_weight.shape[0]
    segments = inputs.shape[0]
    device = lax.axis_index("mp")
    place, core = device // 2, device % 2
    start = core * OWN
    valid_count = lax.psum(jnp.sum(valid_mask.astype(F32)), "dp")
    attention_a = expand(attention_rank < 2, D // attention_rank.shape[2])
    attention_b = expand(attention_rank < 3, D // attention_rank.shape[2])
    feedforward_a = expand(feedforward_rank < 2, D // feedforward_rank.shape[2])
    feedforward_b = expand(feedforward_rank < 3, D // feedforward_rank.shape[2])
    attention_eff = (attention_weight * attention_a).astype(BF16).transpose(0, 1, 3, 2)
    feedforward_eff = (feedforward_weight * feedforward_a).astype(BF16)

    att_all = []
    ff_all = []
    for l in range(layers):
        got = gather_mp(attention_eff[l], place, core)
        att_all.append(got.transpose(1, 0, 2, 3).reshape(5, D, D))
        got = gather_mp(feedforward_eff[l], place, core)
        ff_all.append(got.transpose(1, 0, 2, 3))
    bias_pack = jnp.concatenate(
        [head_bias_weight.reshape(layers, 128), inner_bias_weight], axis=1
    )
    bias_got = gather_mp(bias_pack, place, core)
    bias_all = [
        bias_got[:, l, :128].reshape(MP, 2, HD).transpose(1, 0, 2).reshape(2, D)
        for l in range(layers)
    ]
    inner_bias_all = [bias_got[:, l, 128:].reshape(MP, 1, 256) for l in range(layers)]

    table = lax.dynamic_index_in_dim(tables(), core, 0, False)
    vocab_ids = jnp.arange(VOCAB)
    embedding_low = embedding_weight.astype(BF16)
    onehot_all = (inputs.reshape(-1)[:, None] == vocab_ids[None, :]).astype(BF16)
    memory_zero = dot_nn(onehot_all, embedding_low).astype(BF16).reshape(segments, SEG, D)
    tokens = lax.dynamic_index_in_dim(inputs, place, 0, False)
    own_tokens = lax.dynamic_slice_in_dim(tokens, start, OWN, 0)
    own_targets = lax.dynamic_slice_in_dim(
        lax.dynamic_index_in_dim(targets, place, 0, False), start, OWN, 0
    )
    own_valid = lax.dynamic_slice_in_dim(
        lax.dynamic_index_in_dim(valid_mask, place, 0, False), start, OWN, 0
    ).astype(F32)
    onehot_own = (own_tokens[:, None] == vocab_ids[None, :]).astype(F32)
    hidden = jnp.dot(onehot_own, embedding_weight, precision=lax.Precision.HIGHEST)
    low = lax.dynamic_index_in_dim(memory_zero, place, 0, False)
    own_memory = lax.dynamic_index_in_dim(memory, place, 1, False)
    offset = start.reshape(1)

    states = []
    for l in range(layers):
        if l > 0:
            own_low = hidden.astype(BF16)
            other = lax.ppermute(own_low, "mp", PAIR)
            low = jnp.where(
                core == 0,
                jnp.concatenate([own_low, other]),
                jnp.concatenate([other, own_low]),
            )
            memory_one = gather_mp(own_low, place, core).reshape(segments, SEG, D)
        result = layer_forward(
            offset,
            hidden,
            low,
            own_memory[l],
            att_all[l],
            ff_all[l],
            bias_all[l],
            inner_bias_all[l],
            norm_weight[l],
            table,
        )
        states.append((hidden, low, result[1:]))
        hidden = result[0]

    final_low = hidden.astype(BF16)
    logit_scale = D ** (-0.5)
    logits = dot_nt(final_low, embedding_low) * logit_scale
    onehot_out = (own_targets[:, None] == vocab_ids[None, :]).astype(F32)
    peak = jnp.max(logits, axis=-1, keepdims=True)
    log_total = peak + jnp.log(jnp.sum(jnp.exp(logits - peak), axis=-1, keepdims=True))
    picked = jnp.sum(logits * onehot_out, axis=-1)
    ce_total = lax.psum(jnp.sum(own_valid * (log_total[:, 0] - picked)), ("dp", "mp"))
    grad_logits = (
        own_valid[:, None] * (jnp.exp(logits - log_total) - onehot_out) / valid_count
    ).astype(BF16)
    grad_hidden = dot_nn(grad_logits, embedding_low) * logit_scale
    grad_embedding = (
        lax.dot_general(grad_logits, final_low, (((0,), (0,)), ((), ())), preferred_element_type=F32)
        * logit_scale
    )

    grads = [None] * layers
    for l in reversed(range(layers)):
        layer_hidden, layer_low, saved = states[l]
        grad_own, kept, sent, grad_att, grad_kv, *rest = layer_backward(
            offset,
            grad_hidden,
            layer_hidden,
            layer_low,
            own_memory[l],
            att_all[l],
            ff_all[l],
            inner_bias_all[l],
            norm_weight[l],
            table,
            saved,
        )
        got = lax.ppermute(sent, "mp", PAIR)
        grad_hidden, grad_kv = layer_finish(
            grad_own, kept, got, layer_hidden, att_all[l], grad_kv
        )
        grad_att = jnp.concatenate([grad_att[0:1], grad_kv, grad_att[3:5]])
        grads[l] = (grad_att, *rest)
    grad_embedding = grad_embedding + lax.dot_general(
        onehot_own, grad_hidden, (((0,), (0,)), ((), ())), precision=lax.Precision.HIGHEST
    )

    small = jnp.zeros((MP, 48, D), F32)
    small = small.at[:, 0:32].set(grad_embedding.reshape(MP, 32, D))
    small = small.at[:, 32, 0:256].set(
        jnp.stack([g[2].reshape(2, MP, HD).transpose(1, 0, 2) for g in grads], axis=1).reshape(
            MP, 256
        )
    )
    small = small.at[:, 33].set(
        jnp.stack([g[3].reshape(MP, 256) for g in grads], axis=1).reshape(MP, 512)
    )
    small = small.at[:, 34:36].set(
        jnp.concatenate([g[4] for g in grads], axis=0).reshape(MP, 2, D)
    )
    grad_attention = jnp.stack(
        [scatter_mp(g[0].reshape(5, MP, HD, D).transpose(1, 0, 2, 3), place, core) for g in grads]
    )
    grad_feedforward = jnp.stack(
        [scatter_mp(g[1].transpose(1, 0, 2, 3), place, core) for g in grads]
    )
    grad_small = scatter_mp(small.astype(BF16), place, core)
    grad_attention, grad_feedforward, grad_small = lax.psum(
        (grad_attention.astype(BF16), grad_feedforward.astype(BF16), grad_small.astype(BF16)), "dp"
    )
    small_all = gather_mp(grad_small, place, core).astype(F32)
    grad_embedding = small_all[:, 0:32].reshape(VOCAB, D)
    grad_norm = small_all[:, 34:36].reshape(2, 8, D)[:, 0:5]
    grad_small = grad_small.astype(F32)
    grad_head_bias = grad_small[32, 0:256].reshape(layers, 2, HD)
    grad_inner_bias = grad_small[33].reshape(layers, 256)
    grad_attention = grad_attention.astype(F32).transpose(0, 1, 3, 2)
    grad_feedforward = grad_feedforward.astype(F32)

    attention_coef = attention_a + WIDEN * (attention_b - attention_a)
    feedforward_coef = feedforward_a + WIDEN * (feedforward_b - feedforward_a)
    grad_attention = (
        attention_b * grad_attention + 2.0 * PENALTY * attention_weight * attention_coef
    )
    grad_feedforward = (
        feedforward_b * grad_feedforward + 2.0 * PENALTY * feedforward_weight * feedforward_coef
    )
    groups = [
        (attention_weight, attention_moment, attention_average, grad_attention),
        (feedforward_weight, feedforward_moment, feedforward_average, grad_feedforward),
        (head_bias_weight, head_bias_moment, head_bias_average, grad_head_bias),
        (inner_bias_weight, inner_bias_moment, inner_bias_average, grad_inner_bias),
        (embedding_weight, embedding_moment, embedding_average, grad_embedding),
        (norm_weight, norm_moment, norm_average, grad_norm),
    ]
    moments_next = [MOMENTUM * entry[1] + entry[3] for entry in groups]
    directions = [entry[3] + MOMENTUM * moment for entry, moment in zip(groups, moments_next)]
    local_sums = jnp.stack(
        [jnp.sum(entry[0] * entry[0]) for entry in groups[:4]]
        + [jnp.sum(direction * direction) for direction in directions[:4]]
    )
    totals = lax.psum(local_sums, "mp")
    weight_squares = [totals[i] for i in range(4)] + [
        jnp.sum(entry[0] * entry[0]) for entry in groups[4:]
    ]
    direction_squares = [totals[4 + i] for i in range(4)] + [
        jnp.sum(direction * direction) for direction in directions[4:]
    ]
    results = []
    for i in range(6):
        weight, moment, average, grad = groups[i]
        trust_ratio = jnp.sqrt(weight_squares[i]) / jnp.sqrt(direction_squares[i])
        weight_next = weight - RATE * trust_ratio * directions[i]
        results.append(
            (weight_next, moments_next[i], AVERAGE * average + (1.0 - AVERAGE) * weight_next)
        )
    new_memory = jnp.stack([memory_zero, memory_one])
    return (
        ce_total,
        valid_count,
        new_memory,
        grad_attention,
        *results[0],
        grad_feedforward,
        *results[1],
        *results[4],
        *results[2],
        *results[3],
        grad_norm,
        *results[5],
    )


def solution(mesh):
    rows = P("dp", None)
    matrix = P(None, None, None, "mp")
    split_two = P(None, None, "mp")
    split_one = P(None, "mp")
    whole = P()
    return jax.shard_map(
        body,
        mesh=mesh,
        in_specs=(
            (rows,) * 3
            + (P(None, "dp", None, None),)
            + (matrix,) * 8
            + (whole,) * 3
            + (split_two,) * 3
            + (split_one,) * 3
            + (whole,) * 3
        ),
        out_specs=(
            (whole,) * 2
            + (P(None, "dp", None, None),)
            + (matrix,) * 8
            + (whole,) * 3
            + (split_two,) * 3
            + (split_one,) * 3
            + (whole,) * 4
        ),
        check_vma=False,
    )
```

time: 1880 us -> 836 us (0.44)
  local copies, waits for them, and re-layouts: 821 us -> 151 us
  waiting for transfers between devices: 551 us -> 109 us
  matrix products: 247 us -> 8.55 us
  Pallas kernels: 0 us -> 124 us
  starting transfers between devices: 0.78 us -> 106 us
  blocking collectives: 109 us -> 176 us
    psum x9 -> x1, waiting for transfers between devices: 551 us -> 71.5 us  [body(): lax.psum((grad_attention.astype(BF16), grad_feedforward.astype(BF16), gra...]
    slice x20 -> x13, local copies, waits for them, and re-layouts: 379 us -> 11.1 us  [the longest x4 7.5 us: body(): grad_att = jnp.concatenate([grad_att[0:1], grad_kv, grad_att[3:5]])]
    dot_general x141 -> x6, matrix products: 247 us -> 8.55 us  [the longest x2 2.74 us: dot_nn(): lax.dot_general(a, b, (((1,), (0,)), ((), ())), preferred_element_type=F32)]
    pad x24 -> x0, local copies, waits for them, and re-layouts: 187 us -> none  [the longest x8 184 us: unskew_rows(): padded = jnp.pad(flat, ((0, 0), (query_count - 1, 1)))]
    reshape x64 -> x8, local copies, waits for them, and re-layouts: 150 us -> 1.63 us  [the longest x2 1.34 us: body(): bias_got[:, l, :128].reshape(MP, 2, HD).transpose(1, 0, 2).reshape(2, D)]
    pallas_call x0 -> x6, Pallas kernels: none -> 124 us  [the longest x2 65 us: layer_backward(): pl.pallas_call(backward_kernel, out_shape=[jax.ShapeDtypeStruct(s, t) for...]
    ppermute x0 -> x51, starting transfers between devices: none -> 106 us  [the longest x7 39.4 us: gather_mp(): there = lax.ppermute(here, 'mp', PAIR)]
    psum x2 -> x3, blocking collectives: 95.2 us -> 161 us  [the longest x1 68.5 us: body(): lax.psum(jnp.sum(own_valid * (log_total[:, 0] - picked)), ('dp', 'mp'))]
  transfers between devices with their start and end apart: 9 -> 52, of which waited for: 9 -> 12; matrix products, arithmetic and copies ran while one was open for 3% -> 23% of each run, Pallas kernels for 0% -> 5%
where the time goes in v1:
time: 836 us; the launch traced here: 825 us
  blocking collectives  176 us (21%)
  local copies, waits for them, and re-layouts  151 us (18%)
  other arithmetic  128 us (15%)
  Pallas kernels  124 us (15%)
  waiting for transfers between devices  109 us (13%)
  starting transfers between devices  106 us (13%)
  between operations  23.7 us (3%)
  matrix products  8.55 us (1%)
    psum x1, waiting for transfers between devices, body(): lax.psum((grad_attention.astype(BF16), grad_feedforward.astype(BF16), gra...  71.5 us
    psum x1, blocking collectives, body(): lax.psum(jnp.sum(own_valid * (log_total[:, 0] - picked)), ('dp', 'mp'))  68.5 us
    pallas_call x2, Pallas kernels, layer_backward(): pl.pallas_call(backward_kernel, out_shape=[jax.ShapeDtypeStruct(s, t) for...  65 us
    psum x1, blocking collectives, body(): lax.psum((grad_attention.astype(BF16), grad_feedforward.astype(BF16), gra...  57.8 us
    pallas_call x2, Pallas kernels, layer_forward(): pl.pallas_call(forward_kernel, out_shape=[jax.ShapeDtypeStruct(s, t) for...  48.7 us
    ppermute x7, starting transfers between devices, gather_mp(): there = lax.ppermute(here, 'mp', PAIR)  39.4 us
    rev x14, local copies, waits for them, and re-layouts, gather_mp(): turned = jnp.concatenate([both[::-1], both[:0:-1]])  36.3 us
    psum x1, blocking collectives, body(): valid_count = lax.psum(jnp.sum(valid_mask.astype(F32)), 'dp')  35.1 us
  transfers between devices with their start and end apart: 52, of which 12 were waited for; matrix products, arithmetic and copies ran while one was open for 23% of the time, Pallas kernels for 5%

profile of v1, /device:TPU:1, one launch (start us, length us, event | category | flops | bytes accessed | tf_op | source)
XLA Modules:
  0.0 825.3 jit_solution(11408085862063000410)
XLA Ops:
  41.5 35.1 %psum.43 = f32[]{:T(128)} all-reduce(f32[]{:T(128)} %convert_reduce_fusion), channel_id=1, replica_groups=mesh['dp'=16,'mp'=8] {'dp'}, use_global_device_ids=true, to_apply=%region_6.7 | all-reduce | flops 1 | bytes 8 | tf_op jit(solution)/shard_map/psum | solution.py:490
  89.1 15.9 %collective-permute-start.16 = (bf16[4,5,64,512]{3,2,1,0:T(8,128)(2,1)}, bf16[4,5,64,512]{3,2,1,0:T(8,128)(2,1)}, u32[]{:S(2)}, u32[]{:S(2)}) collective-permute-start(bf16[4,5,64,512]{3,2,1,0:T(8,128)(2,1)} %pad_maximum_fusion.11), channel_id=1, source_target_pairs={{0,1},{1,0},{2,3},{3,2},{4,5},{5,4},{6,7},{7,6},{8,9},{9,8},{10,11... | collective-permute-start | bytes 3932168 | tf_op jit(solution)/shard_map/ppermute | solution.py:438
  110.3 9.2 %collective-permute-start.3 = (bf16[4,5,64,512]{3,2,1,0:T(8,128)(2,1)}, bf16[4,5,64,512]{3,2,1,0:T(8,128)(2,1)}, u32[]{:S(2)}, u32[]{:S(2)}) collective-permute-start(bf16[4,5,64,512]{3,2,1,0:T(8,128)(2,1)} %pad_maximum_fusion.10), channel_id=1, source_target_pairs={{0,1},{1,0},{2,3},{3,2},{4,5},{5,4},{6,7},{7,6},{8,9},{9,8},{10,11... | collective-permute-start | bytes 3932168 | tf_op jit(solution)/shard_map/ppermute | solution.py:438
  122.4 7.3 collective-permute-start.7
  132.4 3.0 pad_maximum_fusion.9
  135.3 3.6 collective-permute-start.20
  144.0 3.5 rev.48
  152.2 3.1 rev.43
  155.3 3.4 pad_maximum_fusion.3
  158.7 3.5 rev.42
  179.3 4.6 rev.44
  183.9 3.7 rev.45
  187.6 3.8 rev.51
  191.3 4.6 rev.50
  196.0 6.9 fusion
  202.9 7.3 copy.69
  210.2 24.4 %layer_forward.2 = (f32[256,512]{1,0:T(8,128)}, f32[8,256,1024]{2,1,0:T(8,128)}, bf16[256,512]{1,0:T(8,128)(2,1)}, bf16[256,512]{1,0:T(8,128)(2,1)}, bf16[256,51...) custom-call(s32[1]{0:T(128)} %bitcast.1.offset_ref, ...), custom_call_target="tpu_custom_call" | custom-call | tf_op jit(solution)/shard_map/layer_forward/pallas_call | solution.py:195
  239.3 3.0 rev.49
  246.8 7.7 copy.75
  256.5 24.4 %layer_forward.3 = (f32[256,512]{1,0:T(8,128)}, f32[8,256,1024]{2,1,0:T(8,128)}, bf16[256,512]{1,0:T(8,128)(2,1)}, bf16[256,512]{1,0:T(8,128)(2,1)}, bf16[256,51...) custom-call(s32[1]{0:T(128)} %bitcast.1.offset_ref, ...), custom_call_target="tpu_custom_call" | custom-call | tf_op jit(solution)/shard_map/layer_forward/pallas_call | solution.py:195
  284.7 32.5 %layer_backward.2 = (f32[256,512]{1,0:T(8,128)}, f32[2,512,256]{2,1,0:T(8,128)}, f32[2,512,256]{2,1,0:T(8,128)}, bf16[5,512,512]{2,1,0:T(8,128)(2,1)}, f32[2,512...) custom-call(s32[1]{0:T(128)} %bitcast.1.offset_ref, ...), custom_call_target="tpu_custom_call" | custom-call | tf_op jit(solution)/shard_map/layer_backward/pallas_call | solution.py:373
  327.3 3.6 collective-permute-start.22
  331.0 68.5 %psum.42 = f32[]{:T(128)} all-reduce(f32[]{:T(128)} %get-tuple-element.211), channel_id=1, replica_groups=mesh['dp'=16,'mp'=8] {'dp','mp'}, use_global_device_ids=true, to_apply=%region_4.5 | all-reduce | flops 1 | bytes 8 | tf_op jit(solution)/shard_map/psum | solution.py:567
  403.7 3.1 dynamic-slice_bitcast_fusion
  411.9 5.1 layer_finish.2
  417.0 32.5 %layer_backward.3 = (f32[256,512]{1,0:T(8,128)}, f32[2,512,256]{2,1,0:T(8,128)}, f32[2,512,256]{2,1,0:T(8,128)}, bf16[5,512,512]{2,1,0:T(8,128)(2,1)}, f32[2,512...) custom-call(s32[1]{0:T(128)} %bitcast.1.offset_ref, ...), custom_call_target="tpu_custom_call" | custom-call | tf_op jit(solution)/shard_map/layer_backward/pallas_call | solution.py:373
  455.5 3.3 dynamic-slice_bitcast_fusion.1
  469.1 3.1 pad_maximum_fusion.7
  472.1 3.0 rev.52
  481.4 5.1 layer_finish.3
  516.8 57.8 %psum.46 = bf16[48,512]{1,0:T(8,128)(2,1)S(1)} all-reduce(bf16[48,512]{1,0:T(8,128)(2,1)S(1)} %fusion.43), channel_id=1, replica_groups=mesh['dp'=16,'mp'=8] {'dp'}, use_global_device_ids=true, to_apply=%region_15.16 | all-reduce | flops 24576 | bytes 98304 | tf_op jit(solution)/shard_map/psum | solution.py:623
  583.2 4.7 collective-permute-start.49
  589.1 18.1 %collective-permute-start.27 = (bf16[4,5,64,512]{3,2,1,0:T(8,128)(2,1)}, bf16[4,5,64,512]{3,2,1,0:T(8,128)(2,1)}, u32[]{:S(2)}, u32[]{:S(2)}) collective-permute-start(bf16[4,5,64,512]{3,2,1,0:T(8,128)(2,1)} %bitcast.321), channel_id=1, source_target_pairs={{0,1},{1,0},{2,3},{3,2},{4,5},{5,4},{6,7},{7,6},{8,9},{9,8},{10,11... | collective-permute-start | bytes 3932168 | tf_op jit(solution)/shard_map/ppermute | solution.py:450
  608.4 3.2 collective-permute-start.33
  619.1 7.3 collective-permute-done.33
  626.7 4.2 fusion.59
  636.3 3.2 collective-permute-start.37
  649.5 11.1 %collective-permute-done.37 = bf16[2,512,256]{1,2,0:T(8,128)(2,1)} collective-permute-done((bf16[2,512,256]{1,2,0:T(8,128)(2,1)}, bf16[2,512,256]{1,2,0:T(8,128)(2,1)}, u32[]{:S(2)}, u32[]{:S(2)}) %collective-permute-start.37) | collective-permute-done | bytes 524320 | tf_op jit(solution)/shard_map/ppermute | solution.py:455
  665.9 3.2 collective-permute-done.28
  669.1 5.5 collective-permute-done.29
  690.0 71.5 %all-reduce.4.cloned.1.call-done = (bf16[2,5,64,512]{3,2,1,0:T(8,128)(2,1)}, bf16[2,2,512,256]{2,3,1,0:T(8,128)(2,1)}) async-done(((bf16[2,5,64,512]{3,2,1,0:T(8,128)(2,1)}, bf16[2,2,512,256]{2,3,1,0:T(8,128)(2,1)}), (bf16[2,5,64,512]{3,2,1,0:T(8,128)(2,1)}, bf16[2,2,512,256]{2,3,1,0:T(8,128)(2,1)})) %all-reduce.4.cloned.1.call-update) | async-done | bytes 1703952 | tf_op jit(solution)/shard_map/psum | solution.py:623
  761.5 3.9 multiply_add_fusion.2
  770.7 5.1 stack.285
  778.7 14.3 %psum.47 = f32[8]{0:T(128)S(1)} all-reduce(f32[8]{0:T(128)S(1)} %stack.285), channel_id=1, replica_groups=mesh['dp'=16,'mp'=8] {'mp'}, use_global_device_ids=true, to_apply=%region_18.19 | all-reduce | flops 8 | bytes 64 | tf_op jit(solution)/shard_map/psum | solution.py:657
  797.7 5.9 multiply_add_fusion
  803.7 3.0 copy.106
  809.9 3.0 copy.107
  814.1 3.8 multiply_add_fusion.3
  (409 shorter events, 235.0 us)
Async XLA Ops:
  7.2 754.2 %all-reduce.4.cloned.1.call-start = ((), (), s32[]{:S(2)}) async-start(), calls=%async_computation | async-start | bytes 3407872 | tf_op jit(solution)/shard_map/psum | solution.py:623
  11.2 67.4 %collective-permute-start.13 = (bf16[5,64,512]{2,1,0:T(8,128)(2,1)}, bf16[5,64,512]{2,1,0:T(8,128)(2,1)}, u32[]{:S(2)}, u32[]{:S(2)}) collective-permute-start(bf16[5,64,512]{2,1,0:T(8,128)(2,1)} %get-tuple-element.252), channel_id=1, source_target_pairs={{0,2},{1,3},{2,4},{3,5},{4,6},{5,7},{6,0},{7,1},{8,10},{9,11},{10,... | collective-permute-start | bytes 983048 | tf_op jit(solution)/shard_map/ppermute | solution.py:437
  13.4 68.7 %collective-permute-start.14 = (bf16[5,64,512]{2,1,0:T(8,128)(2,1)}, bf16[5,64,512]{2,1,0:T(8,128)(2,1)}, u32[]{:S(2)}, u32[]{:S(2)}) collective-permute-start(bf16[5,64,512]{2,1,0:T(8,128)(2,1)} %get-tuple-element.252), channel_id=1, source_target_pairs={{0,4},{1,5},{2,6},{3,7},{4,0},{5,1},{6,2},{7,3},{8,12},{9,13},{10,... | collective-permute-start | bytes 983048 | tf_op jit(solution)/shard_map/ppermute | solution.py:437
  16.7 18.6 %collective-permute-start.8 = (f32[2,384]{1,0:T(2,128)S(1)}, f32[2,384]{1,0:T(2,128)S(1)}, u32[]{:S(2)}, u32[]{:S(2)}) collective-permute-start(f32[2,384]{1,0:T(2,128)S(1)} %get-tuple-element.273), channel_id=1, source_target_pairs={{0,2},{1,3},{2,4},{3,5},{4,6},{5,7},{6,0},{7,1},{8,10},{9,11},{10,... | collective-permute-start | bytes 9224 | tf_op jit(solution)/shard_map/ppermute | solution.py:437
  16.7 19.2 %collective-permute-start.9 = (f32[2,384]{1,0:T(2,128)S(1)}, f32[2,384]{1,0:T(2,128)S(1)}, u32[]{:S(2)}, u32[]{:S(2)}) collective-permute-start(f32[2,384]{1,0:T(2,128)S(1)} %get-tuple-element.273), channel_id=1, source_target_pairs={{0,4},{1,5},{2,6},{3,7},{4,0},{5,1},{6,2},{7,3},{8,12},{9,13},{10,... | collective-permute-start | bytes 9224 | tf_op jit(solution)/shard_map/ppermute | solution.py:437
  19.0 19.2 %collective-permute-start.10 = (f32[2,384]{1,0:T(2,128)S(1)}, f32[2,384]{1,0:T(2,128)S(1)}, u32[]{:S(2)}, u32[]{:S(2)}) collective-permute-start(f32[2,384]{1,0:T(2,128)S(1)} %get-tuple-element.273), channel_id=1, source_target_pairs={{0,6},{1,7},{2,0},{3,1},{4,2},{5,3},{6,4},{7,5},{8,14},{9,15},{10,... | collective-permute-start | bytes 9224 | tf_op jit(solution)/shard_map/ppermute | solution.py:437
  35.3 47.2 %collective-permute-start.15 = (bf16[5,64,512]{2,1,0:T(8,128)(2,1)}, bf16[5,64,512]{2,1,0:T(8,128)(2,1)}, u32[]{:S(2)}, u32[]{:S(2)}) collective-permute-start(bf16[5,64,512]{2,1,0:T(8,128)(2,1)} %get-tuple-element.252), channel_id=1, source_target_pairs={{0,6},{1,7},{2,0},{3,1},{4,2},{5,3},{6,4},{7,5},{8,14},{9,15},{10,... | collective-permute-start | bytes 983048 | tf_op jit(solution)/shard_map/ppermute | solution.py:437
  35.9 49.4 %collective-permute-start.1 = (bf16[5,64,512]{2,1,0:T(8,128)(2,1)}, bf16[5,64,512]{2,1,0:T(8,128)(2,1)}, u32[]{:S(2)}, u32[]{:S(2)}) collective-permute-start(bf16[5,64,512]{2,1,0:T(8,128)(2,1)} %get-tuple-element.251), channel_id=1, source_target_pairs={{0,4},{1,5},{2,6},{3,7},{4,0},{5,1},{6,2},{7,3},{8,12},{9,13},{10,... | collective-permute-start | bytes 983048 | tf_op jit(solution)/shard_map/ppermute | solution.py:437
  38.1 39.7 %collective-permute-start.11 = (f32[4,2,384]{2,1,0:T(2,128)S(1)}, f32[4,2,384]{2,1,0:T(2,128)S(1)}, u32[]{:S(2)}, u32[]{:S(2)}) collective-permute-start(f32[4,2,384]{2,1,0:T(2,128)S(1)} %pad_maximum_fusion.21), channel_id=1, source_target_pairs={{0,1},{1,0},{2,3},{3,2},{4,5},{5,4},{6,7},{7,6},{8,9},{9,8},{10,11... | collective-permute-start | bytes 36872 | tf_op jit(solution)/shard_map/ppermute | solution.py:438
  77.9 9.8 %collective-permute-start.2 = (bf16[5,64,512]{2,1,0:T(8,128)(2,1)}, bf16[5,64,512]{2,1,0:T(8,128)(2,1)}, u32[]{:S(2)}, u32[]{:S(2)}) collective-permute-start(bf16[5,64,512]{2,1,0:T(8,128)(2,1)} %get-tuple-element.251), channel_id=1, source_target_pairs={{0,6},{1,7},{2,0},{3,1},{4,2},{5,3},{6,4},{7,5},{8,14},{9,15},{10,... | collective-permute-start | bytes 983048 | tf_op jit(solution)/shard_map/ppermute | solution.py:437
  78.7 10.4 %collective-permute-start = (bf16[5,64,512]{2,1,0:T(8,128)(2,1)}, bf16[5,64,512]{2,1,0:T(8,128)(2,1)}, u32[]{:S(2)}, u32[]{:S(2)}) collective-permute-start(bf16[5,64,512]{2,1,0:T(8,128)(2,1)} %get-tuple-element.251), channel_id=1, source_target_pairs={{0,2},{1,3},{2,4},{3,5},{4,6},{5,7},{6,0},{7,1},{8,10},{9,11},{10,... | collective-permute-start | bytes 983048 | tf_op jit(solution)/shard_map/ppermute | solution.py:437
  82.1 25.5 %collective-permute-start.4 = (bf16[2,512,256]{1,2,0:T(8,128)(2,1)}, bf16[2,512,256]{1,2,0:T(8,128)(2,1)}, u32[]{:S(2)}, u32[]{:S(2)}) collective-permute-start(bf16[2,512,256]{1,2,0:T(8,128)(2,1)} %get-tuple-element.247), channel_id=1, source_target_pairs={{0,2},{1,3},{2,4},{3,5},{4,6},{5,7},{6,0},{7,1},{8,10},{9,11},{10,... | collective-permute-start | bytes 1572872 | tf_op jit(solution)/shard_map/ppermute | solution.py:437
  82.5 27.8 %collective-permute-start.5 = (bf16[2,512,256]{1,2,0:T(8,128)(2,1)}, bf16[2,512,256]{1,2,0:T(8,128)(2,1)}, u32[]{:S(2)}, u32[]{:S(2)}) collective-permute-start(bf16[2,512,256]{1,2,0:T(8,128)(2,1)} %get-tuple-element.247), channel_id=1, source_target_pairs={{0,4},{1,5},{2,6},{3,7},{4,0},{5,1},{6,2},{7,3},{8,12},{9,13},{10,... | collective-permute-start | bytes 1572872 | tf_op jit(solution)/shard_map/ppermute | solution.py:437
  85.2 25.0 %collective-permute-start.6 = (bf16[2,512,256]{1,2,0:T(8,128)(2,1)}, bf16[2,512,256]{1,2,0:T(8,128)(2,1)}, u32[]{:S(2)}, u32[]{:S(2)}) collective-permute-start(bf16[2,512,256]{1,2,0:T(8,128)(2,1)} %get-tuple-element.247), channel_id=1, source_target_pairs={{0,6},{1,7},{2,0},{3,1},{4,2},{5,3},{6,4},{7,5},{8,14},{9,15},{10,... | collective-permute-start | bytes 1572872 | tf_op jit(solution)/shard_map/ppermute | solution.py:437
  87.6 34.7 %collective-permute-start.17 = (bf16[2,512,256]{1,2,0:T(8,128)(2,1)}, bf16[2,512,256]{1,2,0:T(8,128)(2,1)}, u32[]{:S(2)}, u32[]{:S(2)}) collective-permute-start(bf16[2,512,256]{1,2,0:T(8,128)(2,1)} %get-tuple-element.248), channel_id=1, source_target_pairs={{0,2},{1,3},{2,4},{3,5},{4,6},{5,7},{6,0},{7,1},{8,10},{9,11},{10,... | collective-permute-start | bytes 1572872 | tf_op jit(solution)/shard_map/ppermute | solution.py:437
  89.1 49.9 %collective-permute-start.16 = (bf16[4,5,64,512]{3,2,1,0:T(8,128)(2,1)}, bf16[4,5,64,512]{3,2,1,0:T(8,128)(2,1)}, u32[]{:S(2)}, u32[]{:S(2)}) collective-permute-start(bf16[4,5,64,512]{3,2,1,0:T(8,128)(2,1)} %pad_maximum_fusion.11), channel_id=1, source_target_pairs={{0,1},{1,0},{2,3},{3,2},{4,5},{5,4},{6,7},{7,6},{8,9},{9,8},{10,11... | collective-permute-start | bytes 3932168 | tf_op jit(solution)/shard_map/ppermute | solution.py:438
  107.5 24.3 %collective-permute-start.18 = (bf16[2,512,256]{1,2,0:T(8,128)(2,1)}, bf16[2,512,256]{1,2,0:T(8,128)(2,1)}, u32[]{:S(2)}, u32[]{:S(2)}) collective-permute-start(bf16[2,512,256]{1,2,0:T(8,128)(2,1)} %get-tuple-element.248), channel_id=1, source_target_pairs={{0,4},{1,5},{2,6},{3,7},{4,0},{5,1},{6,2},{7,3},{8,12},{9,13},{10,... | collective-permute-start | bytes 1572872 | tf_op jit(solution)/shard_map/ppermute | solution.py:437
  110.3 22.1 %collective-permute-start.19 = (bf16[2,512,256]{1,2,0:T(8,128)(2,1)}, bf16[2,512,256]{1,2,0:T(8,128)(2,1)}, u32[]{:S(2)}, u32[]{:S(2)}) collective-permute-start(bf16[2,512,256]{1,2,0:T(8,128)(2,1)} %get-tuple-element.248), channel_id=1, source_target_pairs={{0,6},{1,7},{2,0},{3,1},{4,2},{5,3},{6,4},{7,5},{8,14},{9,15},{10,... | collective-permute-start | bytes 1572872 | tf_op jit(solution)/shard_map/ppermute | solution.py:437
  110.3 37.2 %collective-permute-start.3 = (bf16[4,5,64,512]{3,2,1,0:T(8,128)(2,1)}, bf16[4,5,64,512]{3,2,1,0:T(8,128)(2,1)}, u32[]{:S(2)}, u32[]{:S(2)}) collective-permute-start(bf16[4,5,64,512]{3,2,1,0:T(8,128)(2,1)} %pad_maximum_fusion.10), channel_id=1, source_target_pairs={{0,1},{1,0},{2,3},{3,2},{4,5},{5,4},{6,7},{7,6},{8,9},{9,8},{10,11... | collective-permute-start | bytes 3932168 | tf_op jit(solution)/shard_map/ppermute | solution.py:438
  122.4 44.1 %collective-permute-start.7 = (bf16[4,2,512,256]{2,3,1,0:T(8,128)(2,1)}, bf16[4,2,512,256]{2,3,1,0:T(8,128)(2,1)}, u32[]{:S(2)}, u32[]{:S(2)}) collective-permute-start(bf16[4,2,512,256]{2,3,1,0:T(8,128)(2,1)} %pad_maximum_fusion.8), channel_id=1, source_target_pairs={{0,1},{1,0},{2,3},{3,2},{4,5},{5,4},{6,7},{7,6},{8,9},{9,8},{10,11... | collective-permute-start | bytes 6291464 | tf_op jit(solution)/shard_map/ppermute | solution.py:438
  135.3 37.6 %collective-permute-start.20 = (bf16[4,2,512,256]{2,3,1,0:T(8,128)(2,1)}, bf16[4,2,512,256]{2,3,1,0:T(8,128)(2,1)}, u32[]{:S(2)}, u32[]{:S(2)}) collective-permute-start(bf16[4,2,512,256]{2,3,1,0:T(8,128)(2,1)} %pad_maximum_fusion.9), channel_id=1, source_target_pairs={{0,1},{1,0},{2,3},{3,2},{4,5},{5,4},{6,7},{7,6},{8,9},{9,8},{10,11... | collective-permute-start | bytes 6291464 | tf_op jit(solution)/shard_map/ppermute | solution.py:438
  236.3 18.2 %collective-permute-start.12 = (bf16[256,512]{1,0:T(8,128)(2,1)}, bf16[256,512]{1,0:T(8,128)(2,1)S(1)}, u32[]{:S(2)}, u32[]{:S(2)}) collective-permute-start(bf16[256,512]{1,0:T(8,128)(2,1)} %convert_element_type.187), channel_id=1, source_target_pairs={{0,1},{1,0},{2,3},{3,2},{4,5},{5,4},{6,7},{7,6},{8,9},{9,8},{10,11... | collective-permute-start | bytes 786440 | tf_op jit(solution)/shard_map/ppermute | solution.py:538
  317.2 94.8 %collective-permute-start.25 = (f32[2,512,256]{2,1,0:T(8,128)}, f32[2,512,256]{2,1,0:T(8,128)}, u32[]{:S(2)}, u32[]{:S(2)}) collective-permute-start(f32[2,512,256]{2,1,0:T(8,128)} %get-tuple-element.124), channel_id=1, source_target_pairs={{0,1},{1,0},{2,3},{3,2},{4,5},{5,4},{6,7},{7,6},{8,9},{9,8},{10,11... | collective-permute-start | bytes 3145736 | tf_op jit(solution)/shard_map/ppermute | solution.py:593
  327.2 80.7 %collective-permute-start.21 = (bf16[256,512]{1,0:T(8,128)(2,1)}, bf16[256,512]{1,0:T(8,128)(2,1)}, u32[]{:S(2)}, u32[]{:S(2)}) collective-permute-start(bf16[256,512]{1,0:T(8,128)(2,1)} %convert_element_type.187), channel_id=1, source_target_pairs={{0,2},{1,3},{2,4},{3,5},{4,6},{5,7},{6,0},{7,1},{8,10},{9,11},{10,... | collective-permute-start | bytes 786440 | tf_op jit(solution)/shard_map/ppermute | solution.py:437
  327.3 80.6 %collective-permute-start.22 = (bf16[256,512]{1,0:T(8,128)(2,1)}, bf16[256,512]{1,0:T(8,128)(2,1)}, u32[]{:S(2)}, u32[]{:S(2)}) collective-permute-start(bf16[256,512]{1,0:T(8,128)(2,1)} %convert_element_type.187), channel_id=1, source_target_pairs={{0,4},{1,5},{2,6},{3,7},{4,0},{5,1},{6,2},{7,3},{8,12},{9,13},{10,... | collective-permute-start | bytes 786440 | tf_op jit(solution)/shard_map/ppermute | solution.py:437
  330.9 77.0 %collective-permute-start.23 = (bf16[256,512]{1,0:T(8,128)(2,1)}, bf16[256,512]{1,0:T(8,128)(2,1)}, u32[]{:S(2)}, u32[]{:S(2)}) collective-permute-start(bf16[256,512]{1,0:T(8,128)(2,1)} %convert_element_type.187), channel_id=1, source_target_pairs={{0,6},{1,7},{2,0},{3,1},{4,2},{5,3},{6,4},{7,5},{8,14},{9,15},{10,... | collective-permute-start | bytes 786440 | tf_op jit(solution)/shard_map/ppermute | solution.py:437
  406.8 86.0 %collective-permute-start.39 = (bf16[4,2,512,256]{3,2,0,1:T(8,128)(2,1)}, bf16[4,2,512,256]{3,2,0,1:T(8,128)(2,1)}, u32[]{:S(2)}, u32[]{:S(2)}) collective-permute-start(bf16[4,2,512,256]{3,2,0,1:T(8,128)(2,1)} %dynamic-slice_bitcast_fusion), channel_id=1, source_target_pairs={{0,1},{1,0},{2,3},{3,2},{4,5},{5,4},{6,7},{7,6},{8,9},{9,8},{10,11... | collective-permute-start | bytes 6291464 | tf_op jit(solution)/shard_map/ppermute | solution.py:450
  410.1 52.0 %collective-permute-start.24 = (bf16[4,256,512]{2,1,0:T(8,128)(2,1)}, bf16[4,256,512]{2,1,0:T(8,128)(2,1)}, u32[]{:S(2)}, u32[]{:S(2)}) collective-permute-start(bf16[4,256,512]{2,1,0:T(8,128)(2,1)} %pad_maximum_fusion.12), channel_id=1, source_target_pairs={{0,1},{1,0},{2,3},{3,2},{4,5},{5,4},{6,7},{7,6},{8,9},{9,8},{10,11... | collective-permute-start | bytes 3145736 | tf_op jit(solution)/shard_map/ppermute | solution.py:438
  455.0 26.4 %collective-permute-start.26 = (f32[2,512,256]{2,1,0:T(8,128)}, f32[2,512,256]{2,1,0:T(8,128)}, u32[]{:S(2)}, u32[]{:S(2)}) collective-permute-start(f32[2,512,256]{2,1,0:T(8,128)} %get-tuple-element.138), channel_id=1, source_target_pairs={{0,1},{1,0},{2,3},{3,2},{4,5},{5,4},{6,7},{7,6},{8,9},{9,8},{10,11... | collective-permute-start | bytes 3145736 | tf_op jit(solution)/shard_map/ppermute | solution.py:593
  458.7 167.9 %collective-permute-start.35 = (bf16[4,2,512,256]{3,2,0,1:T(8,128)(2,1)}, bf16[4,2,512,256]{3,2,0,1:T(8,128)(2,1)}, u32[]{:S(2)}, u32[]{:S(2)}) collective-permute-start(bf16[4,2,512,256]{3,2,0,1:T(8,128)(2,1)} %dynamic-slice_bitcast_fusion.1), channel_id=1, source_target_pairs={{0,1},{1,0},{2,3},{3,2},{4,5},{5,4},{6,7},{7,6},{8,9},{9,8},{10,11... | collective-permute-start | bytes 6291464 | tf_op jit(solution)/shard_map/ppermute | solution.py:450
  461.5 115.3 %collective-permute-start.31 = (bf16[4,5,64,512]{3,2,1,0:T(8,128)(2,1)}, bf16[4,5,64,512]{3,2,1,0:T(8,128)(2,1)}, u32[]{:S(2)}, u32[]{:S(2)}) collective-permute-start(bf16[4,5,64,512]{3,2,1,0:T(8,128)(2,1)} %bitcast.320), channel_id=1, source_target_pairs={{0,1},{1,0},{2,3},{3,2},{4,5},{5,4},{6,7},{7,6},{8,9},{9,8},{10,11... | collective-permute-start | bytes 3932168 | tf_op jit(solution)/shard_map/ppermute | solution.py:450
  499.5 14.3 %collective-permute-start.44 = (bf16[48,512]{1,0:T(8,128)(2,1)S(1)}, bf16[48,512]{1,0:T(8,128)(2,1)S(1)}, u32[]{:S(2)}, u32[]{:S(2)}) collective-permute-start(bf16[48,512]{1,0:T(8,128)(2,1)S(1)} %get-tuple-element.256), channel_id=1, source_target_pairs={{0,2},{1,3},{2,4},{3,5},{4,6},{5,7},{6,0},{7,1},{8,10},{9,11},{10,... | collective-permute-start | bytes 147464 | tf_op jit(solution)/shard_map/ppermute | solution.py:455
  499.6 14.5 %collective-permute-start.45 = (bf16[48,512]{1,0:T(8,128)(2,1)S(1)}, bf16[48,512]{1,0:T(8,128)(2,1)S(1)}, u32[]{:S(2)}, u32[]{:S(2)}) collective-permute-start(bf16[48,512]{1,0:T(8,128)(2,1)S(1)} %get-tuple-element.258), channel_id=1, source_target_pairs={{0,4},{1,5},{2,6},{3,7},{4,0},{5,1},{6,2},{7,3},{8,12},{9,13},{10,... | collective-permute-start | bytes 147464 | tf_op jit(solution)/shard_map/ppermute | solution.py:455
  500.7 15.2 %collective-permute-start.46 = (bf16[48,512]{1,0:T(8,128)(2,1)S(1)}, bf16[48,512]{1,0:T(8,128)(2,1)S(1)}, u32[]{:S(2)}, u32[]{:S(2)}) collective-permute-start(bf16[48,512]{1,0:T(8,128)(2,1)S(1)} %get-tuple-element.257), channel_id=1, source_target_pairs={{0,6},{1,7},{2,0},{3,1},{4,2},{5,3},{6,4},{7,5},{8,14},{9,15},{10,... | collective-permute-start | bytes 147464 | tf_op jit(solution)/shard_map/ppermute | solution.py:455
  513.8 93.4 %collective-permute-start.40 = (bf16[2,512,256]{1,2,0:T(8,128)(2,1)}, bf16[2,512,256]{1,2,0:T(8,128)(2,1)}, u32[]{:S(2)}, u32[]{:S(2)}) collective-permute-start(bf16[2,512,256]{1,2,0:T(8,128)(2,1)} %bitcast.116), channel_id=1, source_target_pairs={{0,2},{1,3},{2,4},{3,5},{4,6},{5,7},{6,0},{7,1},{8,10},{9,11},{10,... | collective-permute-start | bytes 1572872 | tf_op jit(solution)/shard_map/ppermute | solution.py:455
  514.0 94.4 %collective-permute-start.41 = (bf16[2,512,256]{1,2,0:T(8,128)(2,1)}, bf16[2,512,256]{1,2,0:T(8,128)(2,1)}, u32[]{:S(2)}, u32[]{:S(2)}) collective-permute-start(bf16[2,512,256]{1,2,0:T(8,128)(2,1)} %bitcast.117), channel_id=1, source_target_pairs={{0,4},{1,5},{2,6},{3,7},{4,0},{5,1},{6,2},{7,3},{8,12},{9,13},{10,... | collective-permute-start | bytes 1572872 | tf_op jit(solution)/shard_map/ppermute | solution.py:455
  576.9 34.8 %collective-permute-start.42 = (bf16[2,512,256]{1,2,0:T(8,128)(2,1)S(1)}, bf16[2,512,256]{1,2,0:T(8,128)(2,1)S(1)}, u32[]{:S(2)}, u32[]{:S(2)}) collective-permute-start(bf16[2,512,256]{1,2,0:T(8,128)(2,1)S(1)} %bitcast.350), channel_id=1, source_target_pairs={{0,6},{1,7},{2,0},{3,1},{4,2},{5,3},{6,4},{7,5},{8,14},{9,15},{10,... | collective-permute-start | bytes 1572872 | tf_op jit(solution)/shard_map/ppermute | solution.py:455
  589.1 56.2 %collective-permute-start.27 = (bf16[4,5,64,512]{3,2,1,0:T(8,128)(2,1)}, bf16[4,5,64,512]{3,2,1,0:T(8,128)(2,1)}, u32[]{:S(2)}, u32[]{:S(2)}) collective-permute-start(bf16[4,5,64,512]{3,2,1,0:T(8,128)(2,1)} %bitcast.321), channel_id=1, source_target_pairs={{0,1},{1,0},{2,3},{3,2},{4,5},{5,4},{6,7},{7,6},{8,9},{9,8},{10,11... | collective-permute-start | bytes 3932168 | tf_op jit(solution)/shard_map/ppermute | solution.py:450
  607.2 11.3 %collective-permute-start.32 = (bf16[5,64,512]{2,1,0:T(8,128)(2,1)S(1)}, bf16[5,64,512]{2,1,0:T(8,128)(2,1)S(1)}, u32[]{:S(2)}, u32[]{:S(2)}) collective-permute-start(bf16[5,64,512]{2,1,0:T(8,128)(2,1)S(1)} %get-tuple-element.243), channel_id=1, source_target_pairs={{0,2},{1,3},{2,4},{3,5},{4,6},{5,7},{6,0},{7,1},{8,10},{9,11},{10,... | collective-permute-start | bytes 983048 | tf_op jit(solution)/shard_map/ppermute | solution.py:455
  608.4 18.0 %collective-permute-start.33 = (bf16[5,64,512]{2,1,0:T(8,128)(2,1)S(1)}, bf16[5,64,512]{2,1,0:T(8,128)(2,1)S(1)}, u32[]{:S(2)}, u32[]{:S(2)}) collective-permute-start(bf16[5,64,512]{2,1,0:T(8,128)(2,1)S(1)} %get-tuple-element.245), channel_id=1, source_target_pairs={{0,4},{1,5},{2,6},{3,7},{4,0},{5,1},{6,2},{7,3},{8,12},{9,13},{10,... | collective-permute-start | bytes 983048 | tf_op jit(solution)/shard_map/ppermute | solution.py:455
  611.6 14.8 %collective-permute-start.34 = (bf16[5,64,512]{2,1,0:T(8,128)(2,1)S(1)}, bf16[5,64,512]{2,1,0:T(8,128)(2,1)S(1)}, u32[]{:S(2)}, u32[]{:S(2)}) collective-permute-start(bf16[5,64,512]{2,1,0:T(8,128)(2,1)S(1)} %get-tuple-element.244), channel_id=1, source_target_pairs={{0,6},{1,7},{2,0},{3,1},{4,2},{5,3},{6,4},{7,5},{8,14},{9,15},{10,... | collective-permute-start | bytes 983048 | tf_op jit(solution)/shard_map/ppermute | solution.py:455
  618.5 58.8 %collective-permute-start.50 = (bf16[4,48,512]{2,1,0:T(8,128)(2,1)}, bf16[4,48,512]{2,1,0:T(8,128)(2,1)}, u32[]{:S(2)}, u32[]{:S(2)}) collective-permute-start(bf16[4,48,512]{2,1,0:T(8,128)(2,1)} %pad_maximum_fusion.16), channel_id=1, source_target_pairs={{0,1},{1,0},{2,3},{3,2},{4,5},{5,4},{6,7},{7,6},{8,9},{9,8},{10,11... | collective-permute-start | bytes 589832 | tf_op jit(solution)/shard_map/ppermute | solution.py:438
  634.0 15.3 %collective-permute-start.36 = (bf16[2,512,256]{1,2,0:T(8,128)(2,1)}, bf16[2,512,256]{1,2,0:T(8,128)(2,1)}, u32[]{:S(2)}, u32[]{:S(2)}) collective-permute-start(bf16[2,512,256]{1,2,0:T(8,128)(2,1)} %bitcast.353), channel_id=1, source_target_pairs={{0,2},{1,3},{2,4},{3,5},{4,6},{5,7},{6,0},{7,1},{8,10},{9,11},{10,... | collective-permute-start | bytes 1572872 | tf_op jit(solution)/shard_map/ppermute | solution.py:455
  636.3 24.3 %collective-permute-start.37 = (bf16[2,512,256]{1,2,0:T(8,128)(2,1)}, bf16[2,512,256]{1,2,0:T(8,128)(2,1)}, u32[]{:S(2)}, u32[]{:S(2)}) collective-permute-start(bf16[2,512,256]{1,2,0:T(8,128)(2,1)} %bitcast.352), channel_id=1, source_target_pairs={{0,4},{1,5},{2,6},{3,7},{4,0},{5,1},{6,2},{7,3},{8,12},{9,13},{10,... | collective-permute-start | bytes 1572872 | tf_op jit(solution)/shard_map/ppermute | solution.py:455
  640.5 22.7 %collective-permute-start.38 = (bf16[2,512,256]{1,2,0:T(8,128)(2,1)}, bf16[2,512,256]{1,2,0:T(8,128)(2,1)S(1)}, u32[]{:S(2)}, u32[]{:S(2)}) collective-permute-start(bf16[2,512,256]{1,2,0:T(8,128)(2,1)} %bitcast.351), channel_id=1, source_target_pairs={{0,6},{1,7},{2,0},{3,1},{4,2},{5,3},{6,4},{7,5},{8,14},{9,15},{10,... | collective-permute-start | bytes 1572872 | tf_op jit(solution)/shard_map/ppermute | solution.py:455
  647.7 21.4 %collective-permute-start.28 = (bf16[5,64,512]{2,1,0:T(8,128)(2,1)S(1)}, bf16[5,64,512]{2,1,0:T(8,128)(2,1)S(1)}, u32[]{:S(2)}, u32[]{:S(2)}) collective-permute-start(bf16[5,64,512]{2,1,0:T(8,128)(2,1)S(1)} %get-tuple-element.240), channel_id=1, source_target_pairs={{0,2},{1,3},{2,4},{3,5},{4,6},{5,7},{6,0},{7,1},{8,10},{9,11},{10,... | collective-permute-start | bytes 983048 | tf_op jit(solution)/shard_map/ppermute | solution.py:455
  649.3 25.3 %collective-permute-start.29 = (bf16[5,64,512]{2,1,0:T(8,128)(2,1)S(1)}, bf16[5,64,512]{2,1,0:T(8,128)(2,1)S(1)}, u32[]{:S(2)}, u32[]{:S(2)}) collective-permute-start(bf16[5,64,512]{2,1,0:T(8,128)(2,1)S(1)} %get-tuple-element.242), channel_id=1, source_target_pairs={{0,4},{1,5},{2,6},{3,7},{4,0},{5,1},{6,2},{7,3},{8,12},{9,13},{10,... | collective-permute-start | bytes 983048 | tf_op jit(solution)/shard_map/ppermute | solution.py:455
  660.6 15.5 %collective-permute-start.30 = (bf16[5,64,512]{2,1,0:T(8,128)(2,1)S(1)}, bf16[5,64,512]{2,1,0:T(8,128)(2,1)S(1)}, u32[]{:S(2)}, u32[]{:S(2)}) collective-permute-start(bf16[5,64,512]{2,1,0:T(8,128)(2,1)S(1)} %get-tuple-element.241), channel_id=1, source_target_pairs={{0,6},{1,7},{2,0},{3,1},{4,2},{5,3},{6,4},{7,5},{8,14},{9,15},{10,... | collective-permute-start | bytes 983048 | tf_op jit(solution)/shard_map/ppermute | solution.py:455
  (77 other events, 1271.5 us)
Sparse Core Ops, SparseCore 0:
  677.4 84.0 all-reduce.3
